TPU v7x, 512 devices: a whole 4x4x16 slice. The times are simulated.
512 devices in a mesh: rows: 64 (over x, z), cols: 8 (over y, core).
Axes of the slice: x: 4, y: 4, z: 16, core: 2. Of those that a mesh axis runs over, the one named last changes fastest.
Arguments:
- features: float32 [16, 32768], P(None, ('rows', 'cols')), may hold values from -4 to 4
- targets: float32 [32, 32768], P(None, ('rows', 'cols')), may hold values from -6 to 6
- point_order: int32 [32768], P(('rows', 'cols')), may hold values from 0 to 32767, as said below
- lengthscale: float32 [16], replicated, may hold values from 1 to 1.8
- noise_var: float32 [32], replicated, may hold values from 0.1 to 1
Outputs:
- solution: float32 [32, 32768], P(None, ('rows', 'cols'))
- residual: float32 [32, 32768], P(None, ('rows', 'cols'))
Inputs may be any that keep to these rules, and one draw needn't show every extreme that they name: `point_order`: each aligned block of 512 entries, the k-th one, holds each of the numbers k * 512 to k * 512 + 511 exactly once.
All inputs are finite; a program needn't handle non-finite values.
Results may differ from a plain program's by a relative error of at most 0.0051.
Values may be sent and summed in bfloat16 or wider, within the bound.
No kernel may reach another device: no remote copies, remote signals or barrier semaphores. Data moves between devices by JAX's collectives and lax.ppermute only.
A program may use at most 64 MiB of HBM per device.

v0:
```python
import math

import jax
import jax.numpy as jnp
from jax import lax
from jax.sharding import Mesh
from jax.sharding import PartitionSpec as P

INNER = 3
OUTER = 2
COLS = ("cols_0", "cols_1")
ROWS = ("rows_0", "rows_1")
ROWS_COLS = ("rows_0", "rows_1", "cols_0", "cols_1")


def rows_first(arrays, axis, dims):
    turned = [jnp.moveaxis(a, dim, 0) for a, dim in zip(arrays, dims)]
    both = jnp.concatenate([t.reshape(len(t), -1) for t in turned], axis=1)
    whole, at, done = (lax.all_gather(both, axis, axis=0, tiled=True), 0, [])
    for t, dim in zip(turned, dims):
        slab = whole[:, at : at + t[0].size].reshape(-1, *t.shape[1:])
        done.append(jnp.moveaxis(slab, 0, dim))
        at += t[0].size
    return tuple(done)


def in_order(parts, dim):
    lengths = list(parts.shape[1:])
    lengths[dim] *= parts.shape[0]
    return jnp.moveaxis(parts, 0, dim).reshape(lengths)


def copy_for_each(array, axis):
    copies = jnp.broadcast_to(array, (lax.axis_size(axis), *array.shape))
    return lax.all_to_all(copies, axis, split_axis=0, concat_axis=0, tiled=True)


def collect(array, axis, dim):
    return in_order(copy_for_each(array, axis), dim)


def in_blocks(array, dim, devices):
    lengths = array.shape
    parts = array.reshape(*lengths[:dim], devices, lengths[dim] // devices, *lengths[dim + 1 :])
    return jnp.moveaxis(parts, dim, 0)


def summed_on_arrival(array, axis, dim):
    parts = in_blocks(array, dim, lax.axis_size(axis))
    arrived = lax.all_to_all(parts, axis, split_axis=0, concat_axis=0, tiled=True)
    return arrived.sum(axis=0)


def taken_together(array, axis):
    return copy_for_each(array, axis).sum(axis=0)


def over_axes(array, axes):
    far, near = axes
    nearer = taken_together(array, near)
    return taken_together(nearer, far)


def in_one(arrays, axis):
    ends = [0]
    for a in arrays:
        ends.append(ends[-1] + a.size)
    total = over_axes(jnp.concatenate([a.ravel() for a in arrays]), axis)
    return tuple((total[b:e].reshape(a.shape) for a, b, e in zip(arrays, ends, ends[1:])))


def kernel_tile(col_feat, col_norm, row_feat, row_norm):
    inner_prod = jnp.dot(
        col_feat.T, row_feat, precision=lax.Precision.HIGHEST, preferred_element_type=jnp.float32
    )
    return jnp.exp(-0.5 * (col_norm[:, None] + row_norm[None, :] - 2.0 * inner_prod)).astype(
        jnp.bfloat16
    )


def apply_columns(running, portion, col_feat, col_norm, row_feat, row_norm):
    columns = portion.shape[1]
    sub_cols = math.gcd(columns, 512)

    def advance(which, summed):
        offset = which * sub_cols
        part_feat = lax.dynamic_slice_in_dim(col_feat, offset, sub_cols, 1)
        part_norm = lax.dynamic_slice_in_dim(col_norm, offset, sub_cols, 0)
        part_vec = lax.dynamic_slice_in_dim(portion, offset, sub_cols, 1)
        kern_tile = kernel_tile(part_feat, part_norm, row_feat, row_norm)
        return summed + jnp.dot(part_vec, kern_tile, preferred_element_type=jnp.float32)

    return lax.fori_loop(0, columns // sub_cols, advance, running)


def body(features, targets, point_order, lengthscale, noise_var):
    scaled = features / lengthscale[:, None]
    block_feat, block_targ = rows_first((scaled, targets), COLS, (1, 1))
    block_norms = jnp.sum(block_feat * block_feat, 0)
    block_first = lax.axis_index(ROWS) * block_feat.shape[1]
    residual = jnp.take(block_targ, point_order - block_first, axis=1)
    noise_col = noise_var[:, None]
    own_len = scaled.shape[1]
    col_feat = collect(scaled, ROWS, 1)
    col_norm = jnp.sum(col_feat * col_feat, 0)
    solution = jnp.zeros_like(residual)
    for outer_turn in range(OUTER):
        remains = collect(residual, COLS, 1)
        res_norm = jnp.sum(remains * remains, 1)
        direction = remains
        correction = jnp.zeros_like(remains)
        for inner_turn in range(INNER):
            block_packed = direction.astype(jnp.bfloat16)
            blank_block = jnp.zeros(block_packed.shape, jnp.float32)
            applied = (
                apply_columns(
                    blank_block, block_packed, block_feat, block_norms, block_feat, block_norms
                )
                + noise_col * direction
            )
            curvature = jnp.sum(direction * applied, 1)
            step_len = res_norm / curvature
            correction = correction + step_len[:, None] * direction
            remains = remains - step_len[:, None] * applied
            if inner_turn + 1 < INNER:
                new_norm = jnp.sum(remains * remains, 1)
                direction = remains + (new_norm / res_norm)[:, None] * direction
                res_norm = new_norm
        correction = lax.dynamic_slice_in_dim(
            correction, lax.axis_index(COLS) * own_len, own_len, 1
        )
        packed = correction.astype(jnp.bfloat16)
        blank = jnp.zeros((packed.shape[0], block_feat.shape[1]), jnp.float32)
        partial_sum = apply_columns(
            blank, collect(packed, ROWS, 1), col_feat, col_norm, block_feat, block_norms
        )
        applied = summed_on_arrival(partial_sum, COLS, 1) + noise_col * correction
        cross_term, energy = in_one(
            (jnp.sum(residual * applied, 1), jnp.sum(applied * applied, 1)),
            (("rows_0", "rows_1"), ("cols_0", "cols_1")),
        )
        damping_w = cross_term / (energy + 1e-06)
        solution = solution + damping_w[:, None] * correction
        residual = residual - damping_w[:, None] * applied
    return (solution, residual)


def solution(mesh):
    finer = Mesh(mesh.devices.reshape(4, 16, 4, 2), ("rows_0", "rows_1", "cols_0", "cols_1"))
    in_specs = (P(None, ROWS_COLS), P(None, ROWS_COLS), P(ROWS_COLS), P(), P())
    out_specs = (P(None, ROWS_COLS), P(None, ROWS_COLS))
    return jax.shard_map(body, mesh=finer, in_specs=in_specs, out_specs=out_specs, check_vma=False)
```

profile of v0, /device:TPU:1, one launch (start us, length us, event | category | flops | bytes accessed | tf_op | source)
XLA Modules:
  0.0 232.1 jit_solution(16867938194832255773)
XLA Ops:
  0.7 0.6 copy-done.4
  1.4 19.5 %all-gather = f32[8,64,48]{1,2,0:T(8,128)S(1)} all-gather(f32[1,64,48]{1,2,0:T(8,128)S(1)} %maximum_bitcast_fusion), channel_id=1, replica_groups=mesh['rows_0'=4,'rows_1'=16,'cols_0'=4,'cols_1'=2] {'cols_0','cols_1'}, dimensions={0}, use_global_device_ids=true | all-gather | bytes 110592 | tf_op jit(solution)/shard_map/all_gather | solution.py:19
  21.2 0.6 gather_fusion
  21.9 0.7 reshape.125
  22.6 3.4 %all-to-all-start = ((f32[8,1,2048]{2,1,0:T(1,128)}), f32[8,1,2048]{2,1,0:T(1,128)S(1)}, u32[]{:S(2)}, u32[]{:S(2)}) async-start(f32[8,1,2048]{2,1,0:T(1,128)} %reshape.125), calls=%async_computation | async-start | bytes 131072 | tf_op jit(solution)/shard_map/all_to_all | solution.py:35
  26.2 1.1 fusion.19
  27.4 1.0 reshape.129
  28.5 2.4 %all-to-all-done = f32[8,1,2048]{2,1,0:T(1,128)S(1)} async-done(((f32[8,1,2048]{2,1,0:T(1,128)}), f32[8,1,2048]{2,1,0:T(1,128)S(1)}, u32[]{:S(2)}, u32[]{:S(2)}) %all-to-all-start) | async-done | bytes 65568 | tf_op jit(solution)/shard_map/all_to_all | solution.py:35
  30.9 13.9 %all-to-all-start.2 = ((f32[64,1,1024]{2,1,0:T(1,128)}), f32[64,1,1024]{2,1,0:T(1,128)S(1)}, u32[]{:S(2)}, u32[]{:S(2)}) async-start(f32[64,1,1024]{2,1,0:T(1,128)} %reshape.129), calls=%async_computation.2 | async-start | bytes 524288 | tf_op jit(solution)/shard_map/all_to_all | solution.py:35
  45.4 0.8 reduce.7
  46.6 0.6 copy-done
  48.9 1.0 reshape.127
  49.9 14.0 %all-to-all-done.2 = f32[64,1,1024]{2,1,0:T(1,128)S(1)} async-done(((f32[64,1,1024]{2,1,0:T(1,128)}), f32[64,1,1024]{2,1,0:T(1,128)S(1)}, u32[]{:S(2)}, u32[]{:S(2)}) %all-to-all-start.2) | async-done | bytes 262176 | tf_op jit(solution)/shard_map/all_to_all | solution.py:35
  63.9 7.7 %all-to-all-start.1 = ((bf16[64,2,1024]{2,1,0:T(2,128)(2,1)}), bf16[64,2,1024]{2,1,0:T(2,128)(2,1)S(1)}, u32[]{:S(2)}, u32[]{:S(2)}) async-start(bf16[64,2,1024]{2,1,0:T(2,128)(2,1)} %reshape.127), calls=%async_computation.1 | async-start | bytes 524288 | tf_op jit(solution)/shard_map/all_to_all | solution.py:35
  71.7 1.3 reduce.8
  73.7 16.6 %all-to-all-done.1 = bf16[64,2,1024]{2,1,0:T(2,128)(2,1)S(1)} async-done(((bf16[64,2,1024]{2,1,0:T(2,128)(2,1)}), bf16[64,2,1024]{2,1,0:T(2,128)(2,1)S(1)}, u32[]{:S(2)}, u32[]{:S(2)}) %all-to-all-start.1) | async-done | bytes 262176 | tf_op jit(solution)/shard_map/all_to_all | solution.py:35
  91.3 12.1 %while.18 = (s32[]{:T(128)}, f32[32,512]{1,0:T(8,128)S(1)}, bf16[32,4096]{1,0:T(8,128)(2,1)S(1)}, f32[4096]{0:T(1024)S(1)}, f32[512]{0:T(512)S(1)}, /*index=5*/f...) while((s32[]{:T(128)}, f32[32,512]{1,0:T(8,128)S(1)}, ...), condition=%wide.region_9.10_spmd.clone, body=%wide.region_8.9_spmd.clone.sunk | while | flops 68452352 | bytes 1286329 | solution.py:93
  91.4 1.2 fusion.64
  92.9 1.2 fusion.64
  94.4 1.2 fusion.64
  95.9 1.2 fusion.64
  97.4 1.2 fusion.64
  98.9 1.2 fusion.64
  100.4 1.2 fusion.64
  101.9 1.2 fusion.64
  103.6 10.5 %all_to_all.59 = f32[8,1,2048]{2,1,0:T(1,128)S(1)} all-to-all(f32[8,1,2048]{2,1,0:T(1,128)S(1)} %reshape.131), channel_id=1, replica_groups=mesh['rows_0'=4,'rows_1'=16,'cols_0'=4,'cols_1'=2] {'cols_0','cols_1'}, dimensions={0} | all-to-all | bytes 131072 | tf_op jit(solution)/shard_map/all_to_all | solution.py:50
  114.1 0.8 reduce.9
  115.3 7.7 %all_to_all.60 = f32[8,1,64]{2,1,0:T(1,128)S(1)} all-to-all(f32[8,1,64]{2,1,0:T(1,128)S(1)} %broadcast_in_dim.101), channel_id=1, replica_groups=mesh['rows_0'=4,'rows_1'=16,'cols_0'=4,'cols_1'=2] {'cols_0','cols_1'}, dimensions={0} | all-to-all | bytes 4096 | tf_op jit(solution)/shard_map/all_to_all | solution.py:35
  123.0 19.3 %all_to_all.61 = f32[64,1,64]{2,1,0:T(1,128)S(1)} all-to-all(f32[64,1,64]{2,1,0:T(1,128)S(1)} %broadcast_in_dim.102), channel_id=1, replica_groups=mesh['rows_0'=4,'rows_1'=16,'cols_0'=4,'cols_1'=2] {'rows_0','rows_1'}, dimensions={0} | all-to-all | bytes 32768 | tf_op jit(solution)/shard_map/all_to_all | solution.py:35
  142.7 9.3 %all_to_all.62 = f32[8,1,2048]{2,1,0:T(1,128)S(1)} all-to-all(f32[8,1,2048]{2,1,0:T(1,128)S(1)} %reshape.133), channel_id=1, replica_groups=mesh['rows_0'=4,'rows_1'=16,'cols_0'=4,'cols_1'=2] {'cols_0','cols_1'}, dimensions={0} | all-to-all | bytes 131072 | tf_op jit(solution)/shard_map/all_to_all | solution.py:35
  152.0 0.8 reduce.10
  154.9 1.0 reshape.135
  155.9 4.6 %all-to-all-start.7 = ((bf16[64,2,1024]{2,1,0:T(2,128)(2,1)}), bf16[64,2,1024]{2,1,0:T(2,128)(2,1)S(1)}, u32[]{:S(2)}, u32[]{:S(2)}) async-start(bf16[64,2,1024]{2,1,0:T(2,128)(2,1)} %reshape.135), calls=%async_computation.7 | async-start | bytes 524288 | tf_op jit(solution)/shard_map/all_to_all | solution.py:35
  160.6 19.8 %all-to-all-done.7 = bf16[64,2,1024]{2,1,0:T(2,128)(2,1)S(1)} async-done(((bf16[64,2,1024]{2,1,0:T(2,128)(2,1)}), bf16[64,2,1024]{2,1,0:T(2,128)(2,1)S(1)}, u32[]{:S(2)}, u32[]{:S(2)}) %all-to-all-start.7) | async-done | bytes 262176 | tf_op jit(solution)/shard_map/all_to_all | solution.py:35
  181.3 12.1 %while.19 = (s32[]{:T(128)}, f32[32,512]{1,0:T(8,128)S(1)}, bf16[32,4096]{1,0:T(8,128)(2,1)S(1)}, f32[4096]{0:T(1024)S(1)}, f32[512]{0:T(512)S(1)}, /*index=5*/f...) while((s32[]{:T(128)}, f32[32,512]{1,0:T(8,128)S(1)}, ...), condition=%wide.region_22.23_spmd.clone, body=%wide.region_21.22_spmd.clone.sunk | while | flops 68452352 | bytes 1286329 | solution.py:93
  181.4 1.2 fusion.69
  182.9 1.2 fusion.69
  184.5 1.2 fusion.69
  186.0 1.2 fusion.69
  187.5 1.2 fusion.69
  189.0 1.2 fusion.69
  190.5 1.2 fusion.69
  192.0 1.2 fusion.69
  193.7 9.4 %all_to_all.63 = f32[8,1,2048]{2,1,0:T(1,128)S(1)} all-to-all(f32[8,1,2048]{2,1,0:T(1,128)S(1)} %reshape.137), channel_id=1, replica_groups=mesh['rows_0'=4,'rows_1'=16,'cols_0'=4,'cols_1'=2] {'cols_0','cols_1'}, dimensions={0} | all-to-all | bytes 131072 | tf_op jit(solution)/shard_map/all_to_all | solution.py:50
  203.1 0.8 reduce.11
  204.2 7.7 %all_to_all.64 = f32[8,1,64]{2,1,0:T(1,128)S(1)} all-to-all(f32[8,1,64]{2,1,0:T(1,128)S(1)} %broadcast_in_dim.105), channel_id=1, replica_groups=mesh['rows_0'=4,'rows_1'=16,'cols_0'=4,'cols_1'=2] {'cols_0','cols_1'}, dimensions={0} | all-to-all | bytes 4096 | tf_op jit(solution)/shard_map/all_to_all | solution.py:35
  212.0 19.3 %all_to_all.65 = f32[64,1,64]{2,1,0:T(1,128)S(1)} all-to-all(f32[64,1,64]{2,1,0:T(1,128)S(1)} %broadcast_in_dim.106), channel_id=1, replica_groups=mesh['rows_0'=4,'rows_1'=16,'cols_0'=4,'cols_1'=2] {'rows_0','rows_1'}, dimensions={0} | all-to-all | bytes 32768 | tf_op jit(solution)/shard_map/all_to_all | solution.py:35
  231.4 0.7 multiply_subtract_fusion.4
  (131 shorter events, 14.3 us)
Async XLA Ops:
  0.6 0.7 copy-start.4
  0.6 0.7 copy-start.1
  0.7 0.7 copy-start.3
  0.7 0.8 copy-start.2
  22.6 8.3 %all-to-all-start = ((f32[8,1,2048]{2,1,0:T(1,128)}), f32[8,1,2048]{2,1,0:T(1,128)S(1)}, u32[]{:S(2)}, u32[]{:S(2)}) async-start(f32[8,1,2048]{2,1,0:T(1,128)} %reshape.125), calls=%async_computation | async-start | bytes 131072 | tf_op jit(solution)/shard_map/all_to_all | solution.py:35
  30.9 33.0 %all-to-all-start.2 = ((f32[64,1,1024]{2,1,0:T(1,128)}), f32[64,1,1024]{2,1,0:T(1,128)S(1)}, u32[]{:S(2)}, u32[]{:S(2)}) async-start(f32[64,1,1024]{2,1,0:T(1,128)} %reshape.129), calls=%async_computation.2 | async-start | bytes 524288 | tf_op jit(solution)/shard_map/all_to_all | solution.py:35
  46.5 0.7 copy-start
  63.9 26.4 %all-to-all-start.1 = ((bf16[64,2,1024]{2,1,0:T(2,128)(2,1)}), bf16[64,2,1024]{2,1,0:T(2,128)(2,1)S(1)}, u32[]{:S(2)}, u32[]{:S(2)}) async-start(bf16[64,2,1024]{2,1,0:T(2,128)(2,1)} %reshape.127), calls=%async_computation.1 | async-start | bytes 524288 | tf_op jit(solution)/shard_map/all_to_all | solution.py:35
  155.9 24.4 %all-to-all-start.7 = ((bf16[64,2,1024]{2,1,0:T(2,128)(2,1)}), bf16[64,2,1024]{2,1,0:T(2,128)(2,1)S(1)}, u32[]{:S(2)}, u32[]{:S(2)}) async-start(bf16[64,2,1024]{2,1,0:T(2,128)(2,1)} %reshape.135), calls=%async_computation.7 | async-start | bytes 524288 | tf_op jit(solution)/shard_map/all_to_all | solution.py:35
where the time goes:
time: 233 us; the launch traced here: 232 us
  blocking collectives  103 us (44%)
  waiting for transfers between devices  52.8 us (23%)
  starting transfers between devices  29.7 us (13%)
  matrix products  25.2 us (11%)
  local copies, waits for them, and re-layouts  11.9 us (5%)
  other arithmetic  8.06 us (3%)
    all_to_all x5, blocking collectives, copy_for_each(): return lax.all_to_all(copies, axis, split_axis=0, concat_axis=0, tiled=True)  63.3 us
    all_to_all x4, waiting for transfers between devices, copy_for_each(): return lax.all_to_all(copies, axis, split_axis=0, concat_axis=0, tiled=True)  52.8 us
    all_to_all x4, starting transfers between devices, copy_for_each(): return lax.all_to_all(copies, axis, split_axis=0, concat_axis=0, tiled=True)  29.7 us
    dot_general x17, matrix products, kernel_tile(): jnp.dot(col_feat.T, row_feat, precision=lax.Precision.HIGHEST, preferred_...  20.1 us
    all_to_all x2, blocking collectives, summed_on_arrival(): lax.all_to_all(parts, axis, split_axis=0, concat_axis=0, tiled=True)  19.9 us
    all_gather x1, blocking collectives, rows_first(): whole, at, done = (lax.all_gather(both, axis, axis=0, tiled=True), 0, [])  19.5 us
    unnamed x25, local copies, waits for them, and re-layouts  6.61 us
    dot_general x22, matrix products, advance(): jnp.dot(part_vec, kern_tile, preferred_element_type=jnp.float32)  5.08 us
  transfers between devices with their start and end apart: 4, of which 4 were waited for; matrix products, arithmetic and copies ran while one was open for 4% of the time, Pallas kernels for 0%

commit v1 on v0

v1 whole, which is shorter than its diff:
```python
import jax
import jax.numpy as jnp
from jax import lax
from jax.experimental import pallas as pl
from jax.experimental.pallas import tpu as pltpu
from jax.sharding import Mesh
from jax.sharding import PartitionSpec as P

INNER = 3
X, Z, Y, K = "rows_0", "rows_1", "cols_0", "cols_1"
ROWS, COLS, PLANE = (X, Z), (Y, K), (X, Y, K)
ROWS_COLS = (X, Z, Y, K)
N_X, N_Z, N_C = 4, 16, 8
FEATS, RHS, OWN, BLOCK = 16, 32, 64, 512
LINE, FLAT = N_Z * OWN, N_X * BLOCK
DEPTH = 7 * FEATS
ROOT_LOG2E = 1.4426950408889634**0.5
F32, BF16 = jnp.float32, jnp.bfloat16
PARAMS = pltpu.CompilerParams(vmem_limit_bytes=40 * 1024 * 1024)


def low_lanes(rows):
    return lax.broadcasted_iota(jnp.int32, (rows, 2 * OWN), 1) < OWN


def join(a, b):
    low = low_lanes(a.shape[0])
    top = jnp.where(low, a, pltpu.roll(b, OWN, 1))
    bottom = jnp.where(low, pltpu.roll(a, OWN, 1), b)
    return jnp.concatenate([top, bottom], axis=0)


def part(field):
    half = field.shape[0] // 2
    top, bottom = field[:half], field[half:]
    low = low_lanes(half)
    return (
        jnp.where(low, top, pltpu.roll(bottom, OWN, 1)),
        jnp.where(low, pltpu.roll(top, OWN, 1), bottom),
    )


def join_all(pieces):
    tiles = [join(a, b) for a, b in zip(pieces[0::2], pieces[1::2])]
    return jnp.concatenate(tiles, axis=1)


def part_all(field):
    pieces = []
    for at in range(0, field.shape[1], 2 * OWN):
        pieces += part(field[:, at : at + 2 * OWN])
    return pieces


def own_piece(pieces):
    me = lax.axis_index(COLS)
    mine = jnp.zeros_like(pieces[0])
    for which, piece in enumerate(pieces):
        mine = jnp.where(me == which, piece, mine)
    return mine


def by_half(column):
    half = column.shape[0] // 2
    return jnp.where(low_lanes(half), column[:half], column[half:])


def three(value):
    first = value.astype(BF16).astype(F32)
    second = (value - first).astype(BF16).astype(F32)
    third = (value - first - second).astype(BF16).astype(F32)
    return first, second, third


def factors(parts, side):
    p1, p2, p3 = parts
    scaled = p1 + (p2 + p3)
    h1, h2, h3 = three(-0.5 * jnp.sum(scaled * scaled, axis=0, keepdims=True))
    row = lax.broadcasted_iota(jnp.int32, scaled.shape, 0)
    at = 0 if side == 0 else 3
    tail = jnp.where(row < 6, 1.0, 0.0)
    for offset, h in enumerate((h1, h2, h3)):
        tail = jnp.where(row == at + offset, h, tail)
    order = (p1, p1, p2, p2, p1, p3) if side == 0 else (p1, p2, p1, p2, p3, p1)
    return jnp.concatenate([*order, tail], axis=0).astype(BF16)


def kernel_of(left, right):
    exponent = lax.dot_general(
        left, right, (((0,), (0,)), ((), ())), preferred_element_type=F32
    )
    return jnp.exp2(exponent).astype(BF16)


def block_cg(residual, kern, noise):
    remains, direction = residual, residual
    correction = jnp.zeros_like(residual)
    res_norm = jnp.sum(remains * remains, axis=1, keepdims=True)
    for turn in range(INNER):
        image = jnp.dot(direction.astype(BF16), kern, preferred_element_type=F32)
        image = image + noise * direction
        step = res_norm / jnp.sum(direction * image, axis=1, keepdims=True)
        correction = correction + step * direction
        remains = remains - step * image
        if turn + 1 < INNER:
            new_norm = jnp.sum(remains * remains, axis=1, keepdims=True)
            direction = remains + (new_norm / res_norm) * direction
            res_norm = new_norm
    return correction


def sums_row(residual, applied):
    lane = lax.broadcasted_iota(jnp.int32, (RHS, 128), 1)
    cross = jnp.sum(residual * applied, axis=1, keepdims=True)
    energy = jnp.sum(applied * applied, axis=1, keepdims=True)
    turned = jnp.where(lane == 0, cross, jnp.where(lane == 1, energy, 0.0)).T
    blank = jnp.zeros((1, 128 - 2 * RHS), F32)
    return jnp.concatenate([turned[0:1], turned[1:2], blank], axis=1)


def damping_of(rows):
    total = jnp.sum(rows, axis=0, keepdims=True)
    turned = jnp.broadcast_to(total, (8, 128)).T
    return turned[0:RHS, 0:1] / (turned[RHS : 2 * RHS, 0:1] + 1e-6)


def pack_body(feat_ref, targ_ref, order_ref, scale_ref, cols_ref, plane_ref):
    def halves(field):
        half = field.shape[0] // 2
        return jnp.concatenate([field[:half], field[half:]], axis=1)

    scaled = halves(feat_ref[...] / scale_ref[...] * ROOT_LOG2E)
    order = (order_ref[...] % BLOCK).astype(F32)
    order = jnp.concatenate([order, order], axis=1)
    order = jnp.broadcast_to(order, (8, 2 * OWN))
    whole = jnp.concatenate([scaled, halves(targ_ref[...]), order], axis=0)
    for to in range(N_C):
        cols_ref[to] = whole
    for to in range(N_X * N_C):
        plane_ref[to] = scaled


def first_body(recv_ref, noise_ref, msg_ref, kern_ref, res_ref, corr_ref):
    pieces = [recv_ref[i] for i in range(N_C)]
    parts = three(join_all([p[0:8] for p in pieces]))
    kern = kernel_of(factors(parts, 0), factors(parts, 1))
    kern_ref[...] = kern
    low = low_lanes(1)
    order = [
        jnp.where(low, a[24:25], b[24:25]) for a, b in zip(pieces[0::2], pieces[1::2])
    ]
    order = jnp.concatenate(order, axis=1).astype(jnp.int32)
    index = lax.broadcasted_iota(jnp.int32, (BLOCK, BLOCK), 0)
    pick = jnp.where(index == order, 1.0, 0.0).astype(BF16)
    targets = three(join_all([p[8:24] for p in pieces]))
    stack = jnp.concatenate(targets, axis=0).astype(BF16)
    moved = jnp.dot(stack, pick, preferred_element_type=F32)
    residual = moved[0:RHS] + (moved[RHS : 2 * RHS] + moved[2 * RHS :])
    res_ref[...] = residual
    correction = own_piece(part_all(block_cg(residual, kern, noise_ref[...])))
    corr_ref[...] = correction
    mine = three(own_piece([p[0:8] for p in pieces]))
    whole = jnp.concatenate([*mine, correction], axis=0).astype(BF16)
    for to in range(N_Z):
        msg_ref[to] = whole


def spread(msg_ref, at, field):
    for which, piece in enumerate(part_all(field)):
        msg_ref[at + which] = piece


TILE = 256


def build_body(line_ref, plane_ref, msg_ref, kern_ref, left_ref, right_ref):
    line = [line_ref[i].astype(F32) for i in range(N_Z)]
    for p in range(N_Z // 2):
        a, b = line[2 * p], line[2 * p + 1]
        parts = [join(a[i : i + 8], b[i : i + 8]) for i in (0, 8, 16)]
        left_ref[:, pl.ds(128 * p, 128)] = factors(parts, 0)
    for p in range(N_X * N_C // 2):
        parts = three(join(plane_ref[2 * p], plane_ref[2 * p + 1]))
        right_ref[:, pl.ds(128 * p, 128)] = factors(parts, 1)
    corr = join_all([piece[24:40] for piece in line]).astype(BF16)

    def step(i, carry):
        at = pl.multiple_of(i * TILE, TILE)
        kern = kernel_of(left_ref[...], right_ref[:, pl.ds(at, TILE)])
        kern_ref[:, pl.ds(at, TILE)] = kern
        field = jnp.dot(corr, kern, preferred_element_type=F32)
        spread(msg_ref, i * (TILE // OWN), field)
        return carry

    lax.fori_loop(0, FLAT // TILE, step, 0)


def again_body(line_ref, kern_ref, msg_ref):
    corr = join_all([line_ref[i].astype(F32) for i in range(N_Z)]).astype(BF16)

    def step(i, carry):
        at = pl.multiple_of(i * TILE, TILE)
        field = jnp.dot(corr, kern_ref[:, pl.ds(at, TILE)], preferred_element_type=F32)
        spread(msg_ref, i * (TILE // OWN), field)
        return carry

    lax.fori_loop(0, FLAT // TILE, step, 0)


def applied_of(recv_ref, corr_ref, noise_ref):
    total = recv_ref[0]
    for i in range(1, N_X * N_C):
        total = total + recv_ref[i]
    return total + by_half(noise_ref[...]) * corr_ref[...]


def share_body(recv_ref, corr_ref, noise_ref, msg_ref):
    applied = applied_of(recv_ref, corr_ref, noise_ref)
    for to in range(N_C):
        msg_ref[to] = applied


def sums_body(recv_ref, res_ref, msg_ref):
    applied = join_all([recv_ref[i] for i in range(N_C)])
    row = sums_row(res_ref[...], applied)
    msg_ref[...] = jnp.broadcast_to(row, msg_ref.shape)


def second_body(
    rows_ref, recv_ref, res_ref, corr_ref, kern_ref, noise_ref, msg_ref, new_ref, sol_ref, mine_ref
):
    damping = damping_of(rows_ref[...])
    applied = join_all([recv_ref[i] for i in range(N_C)])
    residual = res_ref[...] - damping * applied
    sol_ref[...] = by_half(damping) * corr_ref[...]
    mine_ref[...] = own_piece(part_all(residual))
    correction = own_piece(part_all(block_cg(residual, kern_ref[...], noise_ref[...])))
    new_ref[...] = correction
    whole = correction.astype(BF16)
    for to in range(N_Z):
        msg_ref[to] = whole


def last_sums_body(recv_ref, corr_ref, noise_ref, mine_ref, msg_ref, applied_ref):
    applied = applied_of(recv_ref, corr_ref, noise_ref)
    applied_ref[...] = applied
    row = sums_row(split_halves(mine_ref[...]), split_halves(applied))
    msg_ref[...] = jnp.broadcast_to(row, msg_ref.shape)


def split_halves(field):
    return jnp.concatenate([field[:, :OWN], field[:, OWN:]], axis=0)


def gather_body(recv_ref, msg_ref):
    total = jnp.sum(recv_ref[...], axis=0, keepdims=True)
    msg_ref[...] = jnp.broadcast_to(total, msg_ref.shape)


def end_body(rows_ref, applied_ref, corr_ref, sol_ref, mine_ref, sol_out, res_out):
    damping = by_half(damping_of(rows_ref[...]))
    sol_out[...] = split_halves(sol_ref[...] + damping * corr_ref[...])
    res_out[...] = split_halves(mine_ref[...] - damping * applied_ref[...])


def call(body, outs, *args, scratch=(), name):
    return pl.pallas_call(
        body,
        out_shape=[jax.ShapeDtypeStruct(s, d) for s, d in outs],
        in_specs=[pl.BlockSpec(memory_space=pltpu.VMEM)] * len(args),
        out_specs=[pl.BlockSpec(memory_space=pltpu.VMEM)] * len(outs),
        scratch_shapes=list(scratch),
        compiler_params=PARAMS,
        name=name,
    )(*args)


def swap(array, axis):
    return lax.all_to_all(array, axis, split_axis=0, concat_axis=0, tiled=True)


def body(features, targets, point_order, lengthscale, noise_var):
    noise = noise_var[:, None]
    packed = (OWN // 4, 2 * OWN)
    cols_msg, plane_msg = call(
        pack_body,
        [((N_C, 32, 128), F32), ((N_X * N_C, 8, 128), F32)],
        features,
        targets,
        point_order[None, :],
        lengthscale[:, None],
        name="pack",
    )
    block = swap(cols_msg, COLS)
    plane = swap(plane_msg, PLANE)
    line_msg, kern_b, res, corr = call(
        first_body,
        [
            ((N_Z, 40, 128), BF16),
            ((BLOCK, BLOCK), BF16),
            ((RHS, BLOCK), F32),
            (packed, F32),
        ],
        block,
        noise,
        name="first",
    )
    line = swap(line_msg, Z)
    flat_msg, kern = call(
        build_body,
        [((N_X * N_C, *packed), F32), ((LINE, FLAT), BF16)],
        line,
        plane,
        scratch=[pltpu.VMEM((DEPTH, LINE), BF16), pltpu.VMEM((DEPTH, FLAT), BF16)],
        name="build",
    )
    flat = swap(flat_msg, PLANE)
    (share_msg,) = call(
        share_body, [((N_C, *packed), F32)], flat, corr, noise, name="share"
    )
    shared = swap(share_msg, COLS)
    (sums_msg,) = call(sums_body, [((N_X * N_Z, 128), F32)], shared, res, name="sums")
    sums = swap(sums_msg, ROWS)
    line_msg, corr_2, sol, mine = call(
        second_body,
        [((N_Z, *packed), BF16), (packed, F32), (packed, F32), (packed, F32)],
        sums,
        shared,
        res,
        corr,
        kern_b,
        noise,
        name="second",
    )
    line = swap(line_msg, Z)
    (flat_msg,) = call(
        again_body, [((N_X * N_C, *packed), F32)], line, kern, name="again"
    )
    flat = swap(flat_msg, PLANE)
    near_msg, applied = call(
        last_sums_body,
        [((N_C, 128), F32), (packed, F32)],
        flat,
        corr_2,
        noise,
        mine,
        name="last_sums",
    )
    near = swap(near_msg, COLS)
    (sums_msg,) = call(gather_body, [((N_X * N_Z, 128), F32)], near, name="near")
    sums = swap(sums_msg, ROWS)
    return tuple(
        call(
            end_body,
            [((RHS, OWN), F32)] * 2,
            sums,
            applied,
            corr_2,
            sol,
            mine,
            name="end",
        )
    )


def solution(mesh):
    finer = Mesh(mesh.devices.reshape(N_X, N_Z, 4, 2), ROWS_COLS)
    in_specs = (P(None, ROWS_COLS), P(None, ROWS_COLS), P(ROWS_COLS), P(), P())
    out_specs = (P(None, ROWS_COLS), P(None, ROWS_COLS))
    return jax.shard_map(body, mesh=finer, in_specs=in_specs, out_specs=out_specs, check_vma=False)
```

time: 233 us -> 164 us (0.70)
  waiting for transfers between devices: 52.8 us -> 5.5 us
  blocking collectives: 103 us -> 136 us
  starting transfers between devices: 29.7 us -> 4.36 us
  matrix products: 25.2 us -> 0 us
  Pallas kernels: 0 us -> 12.5 us
  local copies, waits for them, and re-layouts: 11.9 us -> 3.54 us
  other arithmetic: 8.06 us -> 0 us
    all_to_all x7 -> x9, blocking collectives: 83.2 us -> 136 us  [swap(): return lax.all_to_all(array, axis, split_axis=0, concat_axis=0, tiled=True)]
    all_to_all x4 -> x1, waiting for transfers between devices: 52.8 us -> 5.5 us  [swap(): return lax.all_to_all(array, axis, split_axis=0, concat_axis=0, tiled=True)]
    all_to_all x4 -> x1, starting transfers between devices: 29.7 us -> 4.36 us  [swap(): return lax.all_to_all(array, axis, split_axis=0, concat_axis=0, tiled=True)]
    dot_general x39 -> x0, matrix products: 25.2 us -> none  [the longest x17 20.1 us: kernel_tile(): jnp.dot(col_feat.T, row_feat, precision=lax.Precision.HIGHEST, preferred_...]
    all_gather x1 -> x0, blocking collectives: 19.5 us -> none  [rows_first(): whole, at, done = (lax.all_gather(both, axis, axis=0, tiled=True), 0, [])]
    pallas_call x0 -> x10, Pallas kernels: none -> 12.5 us  [call(): pl.pallas_call(body, out_shape=[jax.ShapeDtypeStruct(s, d) for s, d in ou...]
    unnamed x25 -> x6, local copies, waits for them, and re-layouts: 6.61 us -> 2.07 us
    all_to_all x5 -> x0, other arithmetic: 4.46 us -> none  [the longest x3 2.86 us: copy_for_each(): return lax.all_to_all(copies, axis, split_axis=0, concat_axis=0, tiled=True)]
  transfers between devices with their start and end apart: 4 -> 1, of which waited for: 4 -> 1; matrix products, arithmetic and copies ran while one was open for 4% -> 0% of each run, Pallas kernels for 0% -> 1%
where the time goes in v1:
time: 164 us; the launch traced here: 163 us
  blocking collectives  136 us (83%)
  Pallas kernels  12.5 us (8%)
  waiting for transfers between devices  5.5 us (3%)
  starting transfers between devices  4.36 us (3%)
  local copies, waits for them, and re-layouts  3.54 us (2%)
    all_to_all x9, blocking collectives, swap(): return lax.all_to_all(array, axis, split_axis=0, concat_axis=0, tiled=True)  136 us
    pallas_call x10, Pallas kernels, call(): pl.pallas_call(body, out_shape=[jax.ShapeDtypeStruct(s, d) for s, d in ou...  12.5 us
    all_to_all x1, waiting for transfers between devices, swap(): return lax.all_to_all(array, axis, split_axis=0, concat_axis=0, tiled=True)  5.5 us
    all_to_all x1, starting transfers between devices, swap(): return lax.all_to_all(array, axis, split_axis=0, concat_axis=0, tiled=True)  4.36 us
  transfers between devices with their start and end apart: 1, of which 1 were waited for; matrix products, arithmetic and copies ran while one was open for 0% of the time, Pallas kernels for 1%

profile of v1, /device:TPU:1, one launch (start us, length us, event | category | flops | bytes accessed | tf_op | source)
XLA Modules:
  0.0 162.9 jit_solution(9650330499591740864)
XLA Ops:
  0.6 0.7 copy.12.scale_ref
  1.4 0.0 copy-start
  1.4 0.7 copy-done
  2.1 0.0 copy-start.1
  2.1 0.7 copy-done.1
  2.8 0.0 copy-start.2
  2.8 0.7 copy-done.2
  3.4 0.8 pack.1
  4.2 14.4 %all_to_all.68.recv_ref = f32[8,32,128]{2,1,0:T(8,128)S(1)} all-to-all(f32[8,32,128]{2,1,0:T(8,128)S(1)} %get-tuple-element.16), channel_id=1, replica_groups=mesh['rows_0'=4,'rows_1'=16,'cols_0'=4,'cols_1'=2] {'cols_0','cols_1'}, dimensions={0} | all-to-all | bytes 262144 | tf_op jit(solution)/shard_map/all_to_all | solution.py:279
  18.7 4.4 %all-to-all-start.2 = ((f32[32,8,128]{2,1,0:T(8,128)}), f32[32,8,128]{2,1,0:T(8,128)S(1)}, u32[]{:S(2)}, u32[]{:S(2)}) async-start(f32[32,8,128]{2,1,0:T(8,128)} %get-tuple-element.18), calls=%async_computation.2 | async-start | bytes 262144 | tf_op jit(solution)/shard_map/all_to_all | solution.py:279
  23.1 0.7 copy.13.noise_ref
  23.8 1.5 first.1
  25.3 5.5 %all-to-all-done.2.plane_ref = f32[32,8,128]{2,1,0:T(8,128)S(1)} async-done(((f32[32,8,128]{2,1,0:T(8,128)}), f32[32,8,128]{2,1,0:T(8,128)S(1)}, u32[]{:S(2)}, u32[]{:S(2)}) %all-to-all-start.2) | async-done | bytes 131104 | tf_op jit(solution)/shard_map/all_to_all | solution.py:279
  30.8 25.0 %all_to_all.69.line_ref = bf16[16,40,128]{2,1,0:T(8,128)(2,1)S(1)} all-to-all(bf16[16,40,128]{2,1,0:T(8,128)(2,1)S(1)} %get-tuple-element.17), channel_id=1, replica_groups=mesh['rows_0'=4,'rows_1'=16,'cols_0'=4,'cols_1'=2] {'rows_1'}, dimensions={0} | all-to-all | bytes 327680 | tf_op jit(solution)/shard_map/all_to_all | solution.py:279
  55.8 5.1 %build.1 = (f32[32,16,128]{2,1,0:T(8,128)S(1)}, bf16[1024,2048]{1,0:T(8,128)(2,1)S(1)}) custom-call(bf16[16,40,128]{2,1,0:T(8,128)(2,1)S(1)} %all_to_all.69.line_ref, f32[32,8,128]{2,1,0:T(8,128)S(1)} %all-to-all-done.2.plane_ref), custom_call_target="tpu_custom_call" | custom-call | tf_op jit(solution)/shard_map/build/pallas_call | solution.py:267
  60.9 15.6 %all_to_all.70.recv_ref = f32[32,16,128]{2,1,0:T(8,128)S(1)} all-to-all(f32[32,16,128]{2,1,0:T(8,128)S(1)} %get-tuple-element.19), channel_id=1, replica_groups=mesh['rows_0'=4,'rows_1'=16,'cols_0'=4,'cols_1'=2] {'rows_0','cols_0','c..., dimensions={0} | all-to-all | bytes 524288 | tf_op jit(solution)/shard_map/all_to_all | solution.py:279
  76.6 0.1 share.1
  76.7 7.4 %all_to_all.71.recv_ref = f32[8,16,128]{2,1,0:T(8,128)S(1)} all-to-all(f32[8,16,128]{2,1,0:T(8,128)S(1)} %share.1), channel_id=1, replica_groups=mesh['rows_0'=4,'rows_1'=16,'cols_0'=4,'cols_1'=2] {'cols_0','cols_1'}, dimensions={0} | all-to-all | bytes 131072 | tf_op jit(solution)/shard_map/all_to_all | solution.py:279
  84.1 0.3 sums.1
  84.3 19.5 %all_to_all.72 = f32[64,1,128]{2,1,0:T(1,128)S(1)} all-to-all(f32[64,1,128]{2,1,0:T(1,128)S(1)} %bitcast.16), channel_id=1, replica_groups=mesh['rows_0'=4,'rows_1'=16,'cols_0'=4,'cols_1'=2] {'rows_0','rows_1'}, dimensions={0} | all-to-all | bytes 65536 | tf_op jit(solution)/shard_map/all_to_all | solution.py:279
  103.8 1.2 second.1
  105.0 14.3 %all_to_all.73.line_ref = bf16[16,16,128]{2,1,0:T(8,128)(2,1)S(1)} all-to-all(bf16[16,16,128]{2,1,0:T(8,128)(2,1)S(1)} %get-tuple-element.23), channel_id=1, replica_groups=mesh['rows_0'=4,'rows_1'=16,'cols_0'=4,'cols_1'=2] {'rows_1'}, dimensions={0} | all-to-all | bytes 131072 | tf_op jit(solution)/shard_map/all_to_all | solution.py:279
  119.3 2.3 %again.1 = f32[32,16,128]{2,1,0:T(8,128)S(1)} custom-call(bf16[16,16,128]{2,1,0:T(8,128)(2,1)S(1)} %all_to_all.73.line_ref, bf16[1024,2048]{1,0:T(8,128)(2,1)S(1)} %get-tuple-element.24.kern_ref), custom_call_target="tpu_custom_call" | custom-call | tf_op jit(solution)/shard_map/again/pallas_call | solution.py:267
  121.6 15.6 %all_to_all.74.recv_ref = f32[32,16,128]{2,1,0:T(8,128)S(1)} all-to-all(f32[32,16,128]{2,1,0:T(8,128)S(1)} %again.1), channel_id=1, replica_groups=mesh['rows_0'=4,'rows_1'=16,'cols_0'=4,'cols_1'=2] {'rows_0','cols_0','c..., dimensions={0} | all-to-all | bytes 524288 | tf_op jit(solution)/shard_map/all_to_all | solution.py:279
  137.2 0.3 last_sums.1
  137.5 7.2 %all_to_all.75 = f32[8,1,128]{2,1,0:T(1,128)S(1)} all-to-all(f32[8,1,128]{2,1,0:T(1,128)S(1)} %bitcast.20), channel_id=1, replica_groups=mesh['rows_0'=4,'rows_1'=16,'cols_0'=4,'cols_1'=2] {'cols_0','cols_1'}, dimensions={0} | all-to-all | bytes 8192 | tf_op jit(solution)/shard_map/all_to_all | solution.py:279
  144.6 17.4 %all_to_all.76 = f32[64,1,128]{2,1,0:T(1,128)S(1)} all-to-all(f32[64,1,128]{2,1,0:T(1,128)S(1)} %bitcast.18), channel_id=1, replica_groups=mesh['rows_0'=4,'rows_1'=16,'cols_0'=4,'cols_1'=2] {'rows_0','rows_1'}, dimensions={0} | all-to-all | bytes 65536 | tf_op jit(solution)/shard_map/all_to_all | solution.py:279
  162.1 0.9 end.1
  (1 shorter events, 0.0 us)
Async XLA Ops:
  1.4 0.7 copy-start
  2.1 0.7 copy-start.1
  2.8 0.7 copy-start.2
  18.7 12.2 %all-to-all-start.2 = ((f32[32,8,128]{2,1,0:T(8,128)}), f32[32,8,128]{2,1,0:T(8,128)S(1)}, u32[]{:S(2)}, u32[]{:S(2)}) async-start(f32[32,8,128]{2,1,0:T(8,128)} %get-tuple-element.18), calls=%async_computation.2 | async-start | bytes 262144 | tf_op jit(solution)/shard_map/all_to_all | solution.py:279

commit v2 on v1

--- a/solution.py
+++ b/solution.py
@@ -16,7 +16,7 @@
 DEPTH = 7 * FEATS
 ROOT_LOG2E = 1.4426950408889634**0.5
 F32, BF16 = jnp.float32, jnp.bfloat16
-PARAMS = pltpu.CompilerParams(vmem_limit_bytes=40 * 1024 * 1024)
+PARAMS = pltpu.CompilerParams(vmem_limit_bytes=12 * 1024 * 1024)
 
 
 def low_lanes(rows):
@@ -124,24 +124,50 @@
     return turned[0:RHS, 0:1] / (turned[RHS : 2 * RHS, 0:1] + 1e-6)
 
 
-def pack_body(feat_ref, targ_ref, order_ref, scale_ref, cols_ref, plane_ref):
+def pack_body(
+    feat_any, targ_any, order_any, scale_any, noise_any,
+    plane_ref, noise_ref,
+    feat_ref, targ_ref, order_ref, scale_ref, given_ref, sems,
+):
+    pairs = (
+        (scale_any, scale_ref),
+        (noise_any, given_ref),
+        (feat_any, feat_ref),
+        (targ_any, targ_ref),
+        (order_any, order_ref),
+    )
+    copies = [
+        pltpu.make_async_copy(src, dst, sems.at[i]) for i, (src, dst) in enumerate(pairs)
+    ]
+    for copy in copies:
+        copy.start()
+    for copy in copies:
+        copy.wait()
+
     def halves(field):
         half = field.shape[0] // 2
         return jnp.concatenate([field[:half], field[half:]], axis=1)
 
-    scaled = halves(feat_ref[...] / scale_ref[...] * ROOT_LOG2E)
+    def column(source, shape):
+        row = lax.broadcasted_iota(jnp.int32, shape, 0)
+        filled = jnp.zeros(shape, F32)
+        for i in range(shape[0]):
+            filled = jnp.where(row == i, source[i], filled)
+        return filled
+
+    scaled = halves(feat_ref[...] / column(scale_ref, (FEATS, OWN)) * ROOT_LOG2E)
     order = (order_ref[...] % BLOCK).astype(F32)
     order = jnp.concatenate([order, order], axis=1)
     order = jnp.broadcast_to(order, (8, 2 * OWN))
     whole = jnp.concatenate([scaled, halves(targ_ref[...]), order], axis=0)
-    for to in range(N_C):
-        cols_ref[to] = whole
     for to in range(N_X * N_C):
-        plane_ref[to] = scaled
+        plane_ref[to] = whole
+    noise_ref[...] = column(given_ref, (RHS, 128))
 
 
 def first_body(recv_ref, noise_ref, msg_ref, kern_ref, res_ref, corr_ref):
-    pieces = [recv_ref[i] for i in range(N_C)]
+    base = lax.axis_index(X) * N_C
+    pieces = [recv_ref[base + i] for i in range(N_C)]
     parts = three(join_all([p[0:8] for p in pieces]))
     kern = kernel_of(factors(parts, 0), factors(parts, 1))
     kern_ref[...] = kern
@@ -157,7 +183,7 @@
     moved = jnp.dot(stack, pick, preferred_element_type=F32)
     residual = moved[0:RHS] + (moved[RHS : 2 * RHS] + moved[2 * RHS :])
     res_ref[...] = residual
-    correction = own_piece(part_all(block_cg(residual, kern, noise_ref[...])))
+    correction = own_piece(part_all(block_cg(residual, kern, noise_ref[:, 0:1])))
     corr_ref[...] = correction
     mine = three(own_piece([p[0:8] for p in pieces]))
     whole = jnp.concatenate([*mine, correction], axis=0).astype(BF16)
@@ -171,6 +197,7 @@
 
 
 TILE = 256
+STEP = min(LINE, 256)
 
 
 def build_body(line_ref, plane_ref, msg_ref, kern_ref, left_ref, right_ref):
@@ -180,7 +207,7 @@
         parts = [join(a[i : i + 8], b[i : i + 8]) for i in (0, 8, 16)]
         left_ref[:, pl.ds(128 * p, 128)] = factors(parts, 0)
     for p in range(N_X * N_C // 2):
-        parts = three(join(plane_ref[2 * p], plane_ref[2 * p + 1]))
+        parts = three(join(plane_ref[2 * p, 0:8], plane_ref[2 * p + 1, 0:8]))
         right_ref[:, pl.ds(128 * p, 128)] = factors(parts, 1)
     corr = join_all([piece[24:40] for piece in line]).astype(BF16)
 
@@ -195,23 +222,26 @@
     lax.fori_loop(0, FLAT // TILE, step, 0)
 
 
-def again_body(line_ref, kern_ref, msg_ref):
-    corr = join_all([line_ref[i].astype(F32) for i in range(N_Z)]).astype(BF16)
+def apply_body(flat_ref, kern_ref, msg_ref):
+    corr = jnp.concatenate([flat_ref[i].astype(F32) for i in range(N_X)], axis=1)
+    turned = corr.T.astype(BF16)
 
     def step(i, carry):
-        at = pl.multiple_of(i * TILE, TILE)
-        field = jnp.dot(corr, kern_ref[:, pl.ds(at, TILE)], preferred_element_type=F32)
-        spread(msg_ref, i * (TILE // OWN), field)
+        at = pl.multiple_of(i * STEP, STEP)
+        field = jnp.dot(
+            kern_ref[pl.ds(at, STEP), :], turned, preferred_element_type=F32
+        )
+        spread(msg_ref, i * (STEP // OWN), field.T)
         return carry
 
-    lax.fori_loop(0, FLAT // TILE, step, 0)
+    lax.fori_loop(0, LINE // STEP, step, 0)
 
 
 def applied_of(recv_ref, corr_ref, noise_ref):
     total = recv_ref[0]
-    for i in range(1, N_X * N_C):
+    for i in range(1, recv_ref.shape[0]):
         total = total + recv_ref[i]
-    return total + by_half(noise_ref[...]) * corr_ref[...]
+    return total + by_half(noise_ref[:, 0:1]) * corr_ref[...]
 
 
 def share_body(recv_ref, corr_ref, noise_ref, msg_ref):
@@ -234,10 +264,10 @@
     residual = res_ref[...] - damping * applied
     sol_ref[...] = by_half(damping) * corr_ref[...]
     mine_ref[...] = own_piece(part_all(residual))
-    correction = own_piece(part_all(block_cg(residual, kern_ref[...], noise_ref[...])))
-    new_ref[...] = correction
+    correction = block_cg(residual, kern_ref[...], noise_ref[:, 0:1])
+    new_ref[...] = own_piece(part_all(correction))
     whole = correction.astype(BF16)
-    for to in range(N_Z):
+    for to in range(N_X):
         msg_ref[to] = whole
 
 
@@ -263,35 +293,45 @@
     res_out[...] = split_halves(mine_ref[...] - damping * applied_ref[...])
 
 
-def call(body, outs, *args, scratch=(), name):
+def call(body, outs, *args, scratch=(), space=pltpu.VMEM, flops=1 << 20, name):
     return pl.pallas_call(
         body,
         out_shape=[jax.ShapeDtypeStruct(s, d) for s, d in outs],
-        in_specs=[pl.BlockSpec(memory_space=pltpu.VMEM)] * len(args),
+        in_specs=[pl.BlockSpec(memory_space=space)] * len(args),
         out_specs=[pl.BlockSpec(memory_space=pltpu.VMEM)] * len(outs),
         scratch_shapes=list(scratch),
         compiler_params=PARAMS,
+        cost_estimate=pl.CostEstimate(flops=flops, transcendentals=0, bytes_accessed=1 << 20),
         name=name,
     )(*args)
 
 
+def stay(array):
+    return pltpu.with_memory_space_constraint(array, pltpu.HBM)
+
+
 def swap(array, axis):
     return lax.all_to_all(array, axis, split_axis=0, concat_axis=0, tiled=True)
 
 
 def body(features, targets, point_order, lengthscale, noise_var):
-    noise = noise_var[:, None]
-    packed = (OWN // 4, 2 * OWN)
-    cols_msg, plane_msg = call(
+    packed = (RHS // 2, 2 * OWN)
+    n_p = N_X * N_C
+    plane_msg, noise = call(
         pack_body,
-        [((N_C, 32, 128), F32), ((N_X * N_C, 8, 128), F32)],
-        features,
-        targets,
-        point_order[None, :],
-        lengthscale[:, None],
+        [((n_p, 32, 128), F32), ((RHS, 128), F32)],
+        *map(stay, (features, targets, point_order[None, :], lengthscale, noise_var)),
+        scratch=[
+            pltpu.VMEM((FEATS, OWN), F32),
+            pltpu.VMEM((RHS, OWN), F32),
+            pltpu.VMEM((1, OWN), jnp.int32),
+            pltpu.SMEM((FEATS,), F32),
+            pltpu.SMEM((RHS,), F32),
+            pltpu.SemaphoreType.DMA((5,)),
+        ],
+        space=pltpu.HBM,
         name="pack",
     )
-    block = swap(cols_msg, COLS)
     plane = swap(plane_msg, PLANE)
     line_msg, kern_b, res, corr = call(
         first_body,
@@ -301,14 +341,14 @@
             ((RHS, BLOCK), F32),
             (packed, F32),
         ],
-        block,
+        plane,
         noise,
         name="first",
     )
     line = swap(line_msg, Z)
     flat_msg, kern = call(
         build_body,
-        [((N_X * N_C, *packed), F32), ((LINE, FLAT), BF16)],
+        [((n_p, *packed), F32), ((LINE, FLAT), BF16)],
         line,
         plane,
         scratch=[pltpu.VMEM((DEPTH, LINE), BF16), pltpu.VMEM((DEPTH, FLAT), BF16)],
@@ -321,9 +361,9 @@
     shared = swap(share_msg, COLS)
     (sums_msg,) = call(sums_body, [((N_X * N_Z, 128), F32)], shared, res, name="sums")
     sums = swap(sums_msg, ROWS)
-    line_msg, corr_2, sol, mine = call(
+    near_x_msg, corr_2, sol, mine = call(
         second_body,
-        [((N_Z, *packed), BF16), (packed, F32), (packed, F32), (packed, F32)],
+        [((N_X, RHS, BLOCK), BF16), (packed, F32), (packed, F32), (packed, F32)],
         sums,
         shared,
         res,
@@ -332,11 +372,9 @@
         noise,
         name="second",
     )
-    line = swap(line_msg, Z)
-    (flat_msg,) = call(
-        again_body, [((N_X * N_C, *packed), F32)], line, kern, name="again"
-    )
-    flat = swap(flat_msg, PLANE)
+    near_x = swap(near_x_msg, X)
+    (line_msg,) = call(apply_body, [((N_Z, *packed), F32)], near_x, kern, name="apply")
+    flat = swap(line_msg, Z)
     near_msg, applied = call(
         last_sums_body,
         [((N_C, 128), F32), (packed, F32)],

time: 164 us -> 155 us (0.945)
  waiting for transfers between devices: 5.5 us -> 0 us
  blocking collectives: 136 us -> 141 us
  starting transfers between devices: 4.36 us -> 0 us
  local copies, waits for them, and re-layouts: 3.54 us -> 0 us
    all_to_all x1 -> x0, waiting for transfers between devices: 5.5 us -> none  [swap(): return lax.all_to_all(array, axis, split_axis=0, concat_axis=0, tiled=True)]
    all_to_all x9, blocking collectives: 136 us -> 141 us  [swap(): return lax.all_to_all(array, axis, split_axis=0, concat_axis=0, tiled=True)]
    all_to_all x1 -> x0, starting transfers between devices: 4.36 us -> none  [swap(): return lax.all_to_all(array, axis, split_axis=0, concat_axis=0, tiled=True)]
    unnamed x6 -> x0, local copies, waits for them, and re-layouts: 2.07 us -> none
  transfers between devices with their start and end apart: 1 -> 0, of which waited for: 1 -> 0; matrix products, arithmetic and copies ran while one was open for 0% -> 0% of each run, Pallas kernels for 1% -> 0%
where the time goes in v2:
time: 155 us
  blocking collectives  141 us (91%)
  Pallas kernels  12.6 us (8%)
    all_to_all x9, blocking collectives, swap(): return lax.all_to_all(array, axis, split_axis=0, concat_axis=0, tiled=True)  141 us
    pallas_call x10, Pallas kernels, call(): pl.pallas_call(body, out_shape=[jax.ShapeDtypeStruct(s, d) for s, d in ou...  12.6 us

profile of v2, /device:TPU:1, one launch (start us, length us, event | category | flops | bytes accessed | tf_op | source)
XLA Modules:
  0.0 154.6 jit_solution(10370454385233889043)
XLA Ops:
  0.6 0.9 pack.1
  1.6 21.2 %all_to_all.63.recv_ref.plane_ref = f32[32,32,128]{2,1,0:T(8,128)S(1)} all-to-all(f32[32,32,128]{2,1,0:T(8,128)S(1)} %get-tuple-element.16), channel_id=1, replica_groups=mesh['rows_0'=4,'rows_1'=16,'cols_0'=4,'cols_1'=2] {'rows_0','cols_0','c..., dimensions={0} | all-to-all | bytes 1048576 | tf_op jit(solution)/shard_map/all_to_all | solution.py:314
  22.7 1.5 first.1
  24.3 26.4 %all_to_all.64.line_ref = bf16[16,40,128]{2,1,0:T(8,128)(2,1)S(1)} all-to-all(bf16[16,40,128]{2,1,0:T(8,128)(2,1)S(1)} %get-tuple-element.18), channel_id=1, replica_groups=mesh['rows_0'=4,'rows_1'=16,'cols_0'=4,'cols_1'=2] {'rows_1'}, dimensions={0} | all-to-all | bytes 327680 | tf_op jit(solution)/shard_map/all_to_all | solution.py:314
  50.7 5.1 %build.1 = (f32[32,16,128]{2,1,0:T(8,128)S(1)}, bf16[1024,2048]{1,0:T(8,128)(2,1)S(1)}) custom-call(bf16[16,40,128]{2,1,0:T(8,128)(2,1)S(1)} %all_to_all.64.line_ref, f32[32,32,128]{2,1,0:T(8,128)S(1)} %all_to_all.63.recv_ref.plane_ref), custom_call_target="tpu_custom_call" | custom-call | flops 1048576 | bytes 1048576 | tf_op jit(solution)/shard_map/build/pallas_call | solution.py:297
  55.8 15.2 %all_to_all.65.recv_ref = f32[32,16,128]{2,1,0:T(8,128)S(1)} all-to-all(f32[32,16,128]{2,1,0:T(8,128)S(1)} %get-tuple-element.19), channel_id=1, replica_groups=mesh['rows_0'=4,'rows_1'=16,'cols_0'=4,'cols_1'=2] {'rows_0','cols_0','c..., dimensions={0} | all-to-all | bytes 524288 | tf_op jit(solution)/shard_map/all_to_all | solution.py:314
  71.1 0.1 share.1
  71.1 7.4 %all_to_all.66.recv_ref = f32[8,16,128]{2,1,0:T(8,128)S(1)} all-to-all(f32[8,16,128]{2,1,0:T(8,128)S(1)} %share.1), channel_id=1, replica_groups=mesh['rows_0'=4,'rows_1'=16,'cols_0'=4,'cols_1'=2] {'cols_0','cols_1'}, dimensions={0} | all-to-all | bytes 131072 | tf_op jit(solution)/shard_map/all_to_all | solution.py:314
  78.5 0.3 sums.1
  78.8 19.4 %all_to_all.67 = f32[64,1,128]{2,1,0:T(1,128)S(1)} all-to-all(f32[64,1,128]{2,1,0:T(1,128)S(1)} %bitcast.14), channel_id=1, replica_groups=mesh['rows_0'=4,'rows_1'=16,'cols_0'=4,'cols_1'=2] {'rows_0','rows_1'}, dimensions={0} | all-to-all | bytes 65536 | tf_op jit(solution)/shard_map/all_to_all | solution.py:314
  98.2 1.2 second.1
  99.4 7.2 %all_to_all.68.flat_ref = bf16[4,32,512]{2,1,0:T(8,128)(2,1)S(1)} all-to-all(bf16[4,32,512]{2,1,0:T(8,128)(2,1)S(1)} %get-tuple-element.23), channel_id=1, replica_groups=mesh['rows_0'=4,'rows_1'=16,'cols_0'=4,'cols_1'=2] {'rows_0'}, dimensions={0} | all-to-all | bytes 262144 | tf_op jit(solution)/shard_map/all_to_all | solution.py:314
  106.6 2.3 %apply.1 = f32[16,16,128]{2,1,0:T(8,128)S(1)} custom-call(bf16[4,32,512]{2,1,0:T(8,128)(2,1)S(1)} %all_to_all.68.flat_ref, bf16[1024,2048]{1,0:T(8,128)(2,1)S(1)} %get-tuple-element.24.kern_ref), custom_call_target="tpu_custom_call" | custom-call | flops 1048576 | bytes 1048576 | tf_op jit(solution)/shard_map/apply/pallas_call | solution.py:297
  108.9 14.5 %all_to_all.69.recv_ref = f32[16,16,128]{2,1,0:T(8,128)S(1)} all-to-all(f32[16,16,128]{2,1,0:T(8,128)S(1)} %apply.1), channel_id=1, replica_groups=mesh['rows_0'=4,'rows_1'=16,'cols_0'=4,'cols_1'=2] {'rows_1'}, dimensions={0} | all-to-all | bytes 262144 | tf_op jit(solution)/shard_map/all_to_all | solution.py:314
  123.5 0.3 last_sums.1
  123.8 11.7 %all_to_all.70 = f32[8,1,128]{2,1,0:T(1,128)S(1)} all-to-all(f32[8,1,128]{2,1,0:T(1,128)S(1)} %bitcast.18), channel_id=1, replica_groups=mesh['rows_0'=4,'rows_1'=16,'cols_0'=4,'cols_1'=2] {'cols_0','cols_1'}, dimensions={0} | all-to-all | bytes 8192 | tf_op jit(solution)/shard_map/all_to_all | solution.py:314
  135.5 18.3 %all_to_all.71 = f32[64,1,128]{2,1,0:T(1,128)S(1)} all-to-all(f32[64,1,128]{2,1,0:T(1,128)S(1)} %bitcast.16), channel_id=1, replica_groups=mesh['rows_0'=4,'rows_1'=16,'cols_0'=4,'cols_1'=2] {'rows_0','rows_1'}, dimensions={0} | all-to-all | bytes 65536 | tf_op jit(solution)/shard_map/all_to_all | solution.py:314
  153.8 0.9 end.1
  (1 shorter events, 0.0 us)

commit v3 on v2

--- a/solution.py
+++ b/solution.py
@@ -8,7 +8,7 @@
 
 INNER = 3
 X, Z, Y, K = "rows_0", "rows_1", "cols_0", "cols_1"
-ROWS, COLS, PLANE = (X, Z), (Y, K), (X, Y, K)
+PLANE = (X, Y, K)
 ROWS_COLS = (X, Z, Y, K)
 N_X, N_Z, N_C = 4, 16, 8
 FEATS, RHS, OWN, BLOCK = 16, 32, 64, 512
@@ -53,7 +53,7 @@
 
 
 def own_piece(pieces):
-    me = lax.axis_index(COLS)
+    me = lax.axis_index(PLANE)
     mine = jnp.zeros_like(pieces[0])
     for which, piece in enumerate(pieces):
         mine = jnp.where(me == which, piece, mine)
@@ -83,13 +83,6 @@
         tail = jnp.where(row == at + offset, h, tail)
     order = (p1, p1, p2, p2, p1, p3) if side == 0 else (p1, p2, p1, p2, p3, p1)
     return jnp.concatenate([*order, tail], axis=0).astype(BF16)
-
-
-def kernel_of(left, right):
-    exponent = lax.dot_general(
-        left, right, (((0,), (0,)), ((), ())), preferred_element_type=F32
-    )
-    return jnp.exp2(exponent).astype(BF16)
 
 
 def block_cg(residual, kern, noise):
@@ -126,7 +119,7 @@
 
 def pack_body(
     feat_any, targ_any, order_any, scale_any, noise_any,
-    plane_ref, noise_ref,
+    plane_ref, line_ref, noise_ref,
     feat_ref, targ_ref, order_ref, scale_ref, given_ref, sems,
 ):
     pairs = (
@@ -162,33 +155,46 @@
     whole = jnp.concatenate([scaled, halves(targ_ref[...]), order], axis=0)
     for to in range(N_X * N_C):
         plane_ref[to] = whole
+    for to in range(N_Z):
+        line_ref[to] = scaled
     noise_ref[...] = column(given_ref, (RHS, 128))
 
 
-def first_body(recv_ref, noise_ref, msg_ref, kern_ref, res_ref, corr_ref):
-    base = lax.axis_index(X) * N_C
-    pieces = [recv_ref[base + i] for i in range(N_C)]
-    parts = three(join_all([p[0:8] for p in pieces]))
-    kern = kernel_of(factors(parts, 0), factors(parts, 1))
-    kern_ref[...] = kern
-    low = low_lanes(1)
-    order = [
-        jnp.where(low, a[24:25], b[24:25]) for a, b in zip(pieces[0::2], pieces[1::2])
-    ]
-    order = jnp.concatenate(order, axis=1).astype(jnp.int32)
-    index = lax.broadcasted_iota(jnp.int32, (BLOCK, BLOCK), 0)
-    pick = jnp.where(index == order, 1.0, 0.0).astype(BF16)
-    targets = three(join_all([p[8:24] for p in pieces]))
-    stack = jnp.concatenate(targets, axis=0).astype(BF16)
-    moved = jnp.dot(stack, pick, preferred_element_type=F32)
-    residual = moved[0:RHS] + (moved[RHS : 2 * RHS] + moved[2 * RHS :])
-    res_ref[...] = residual
-    correction = own_piece(part_all(block_cg(residual, kern, noise_ref[:, 0:1])))
-    corr_ref[...] = correction
-    mine = three(own_piece([p[0:8] for p in pieces]))
-    whole = jnp.concatenate([*mine, correction], axis=0).astype(BF16)
-    for to in range(N_Z):
-        msg_ref[to] = whole
+def cut(field, which):
+    return field[:, which * BLOCK : (which + 1) * BLOCK]
+
+
+def first_body(
+    recv_ref, noise_ref, kern_ref, state_ref, mine_ref, own_ref, left_ref
+):
+    mine = []
+    residuals = []
+    for x in range(N_X):
+        pieces = [recv_ref[x * N_C + i] for i in range(N_C)]
+        parts = three(join_all([p[0:8] for p in pieces]))
+        left = factors(parts, 0).T
+        left_ref[pl.ds(x * BLOCK, BLOCK), :] = left
+        exponent = jnp.dot(left, factors(parts, 1), preferred_element_type=F32)
+        kern_ref[x] = jnp.exp2(exponent).astype(BF16)
+        low = low_lanes(1)
+        order = [
+            jnp.where(low, a[24:25], b[24:25])
+            for a, b in zip(pieces[0::2], pieces[1::2])
+        ]
+        order = jnp.concatenate(order, axis=1).astype(jnp.int32)
+        index = lax.broadcasted_iota(jnp.int32, (BLOCK, BLOCK), 0)
+        pick = jnp.where(index == order, 1.0, 0.0).astype(BF16)
+        targets = three(join_all([p[8:24] for p in pieces]))
+        stack = jnp.concatenate(targets, axis=0).astype(BF16)
+        moved = jnp.dot(stack, pick, preferred_element_type=F32)
+        residual = moved[0:RHS] + (moved[RHS : 2 * RHS] + moved[2 * RHS :])
+        state_ref[0:RHS, pl.ds(x * BLOCK, BLOCK)] = residual
+        correction = block_cg(residual, kern_ref[x], noise_ref[:, 0:1])
+        state_ref[RHS:, pl.ds(x * BLOCK, BLOCK)] = correction
+        mine += part_all(correction)
+        residuals += part_all(residual)
+    mine_ref[...] = own_piece(mine)
+    own_ref[...] = own_piece(residuals)
 
 
 def spread(msg_ref, at, field):
@@ -196,45 +202,21 @@
         msg_ref[at + which] = piece
 
 
-TILE = 256
-STEP = min(LINE, 256)
-
-
-def build_body(line_ref, plane_ref, msg_ref, kern_ref, left_ref, right_ref):
-    line = [line_ref[i].astype(F32) for i in range(N_Z)]
-    for p in range(N_Z // 2):
-        a, b = line[2 * p], line[2 * p + 1]
-        parts = [join(a[i : i + 8], b[i : i + 8]) for i in (0, 8, 16)]
-        left_ref[:, pl.ds(128 * p, 128)] = factors(parts, 0)
-    for p in range(N_X * N_C // 2):
-        parts = three(join(plane_ref[2 * p, 0:8], plane_ref[2 * p + 1, 0:8]))
-        right_ref[:, pl.ds(128 * p, 128)] = factors(parts, 1)
-    corr = join_all([piece[24:40] for piece in line]).astype(BF16)
-
-    def step(i, carry):
-        at = pl.multiple_of(i * TILE, TILE)
-        kern = kernel_of(left_ref[...], right_ref[:, pl.ds(at, TILE)])
+TILE = min(LINE, 256)
+
+
+def build_body(line_ref, left_ref, state_ref, msg_ref, kern_ref):
+    packed = state_ref[RHS:, :].astype(BF16)
+    for at in range(0, LINE, TILE):
+        tiles = range(at // OWN, (at + TILE) // OWN, 2)
+        field = jnp.concatenate([join(line_ref[i], line_ref[i + 1]) for i in tiles], axis=1)
+        exponent = jnp.dot(
+            left_ref[...], factors(three(field), 1), preferred_element_type=F32
+        )
+        kern = jnp.exp2(exponent).astype(BF16)
         kern_ref[:, pl.ds(at, TILE)] = kern
-        field = jnp.dot(corr, kern, preferred_element_type=F32)
-        spread(msg_ref, i * (TILE // OWN), field)
-        return carry
-
-    lax.fori_loop(0, FLAT // TILE, step, 0)
-
-
-def apply_body(flat_ref, kern_ref, msg_ref):
-    corr = jnp.concatenate([flat_ref[i].astype(F32) for i in range(N_X)], axis=1)
-    turned = corr.T.astype(BF16)
-
-    def step(i, carry):
-        at = pl.multiple_of(i * STEP, STEP)
-        field = jnp.dot(
-            kern_ref[pl.ds(at, STEP), :], turned, preferred_element_type=F32
-        )
-        spread(msg_ref, i * (STEP // OWN), field.T)
-        return carry
-
-    lax.fori_loop(0, LINE // STEP, step, 0)
+        moved = jnp.dot(packed, kern, preferred_element_type=F32)
+        spread(msg_ref, at // OWN, moved)
 
 
 def applied_of(recv_ref, corr_ref, noise_ref):
@@ -246,29 +228,35 @@
 
 def share_body(recv_ref, corr_ref, noise_ref, msg_ref):
     applied = applied_of(recv_ref, corr_ref, noise_ref)
-    for to in range(N_C):
+    for to in range(N_X * N_C):
         msg_ref[to] = applied
 
 
-def sums_body(recv_ref, res_ref, msg_ref):
-    applied = join_all([recv_ref[i] for i in range(N_C)])
-    row = sums_row(res_ref[...], applied)
+def sums_body(recv_ref, res_ref, msg_ref, applied_ref):
+    applied = join_all([recv_ref[i] for i in range(N_X * N_C)])
+    applied_ref[...] = applied
+    row = sums_row(res_ref[0:RHS, :], applied)
     msg_ref[...] = jnp.broadcast_to(row, msg_ref.shape)
 
 
 def second_body(
-    rows_ref, recv_ref, res_ref, corr_ref, kern_ref, noise_ref, msg_ref, new_ref, sol_ref, mine_ref
+    rows_ref, applied_ref, res_ref, block_ref, kern_ref, noise_ref, corr_ref, own_ref, near_ref,
+    msg_ref, new_ref, sol_ref, mine_ref,
 ):
     damping = damping_of(rows_ref[...])
-    applied = join_all([recv_ref[i] for i in range(N_C)])
-    residual = res_ref[...] - damping * applied
+    residual = res_ref[0:RHS, :] - damping * applied_ref[...]
+    corrections = [
+        block_cg(cut(residual, x), block_ref[x], noise_ref[:, 0:1]) for x in range(N_X)
+    ]
+    correction = jnp.concatenate(corrections, axis=1)
+    packed = correction.astype(BF16)
+    for at in range(0, LINE, TILE):
+        moved = jnp.dot(packed, kern_ref[:, pl.ds(at, TILE)], preferred_element_type=F32)
+        spread(msg_ref, at // OWN, moved)
+    new_ref[...] = own_piece(part_all(correction))
     sol_ref[...] = by_half(damping) * corr_ref[...]
-    mine_ref[...] = own_piece(part_all(residual))
-    correction = block_cg(residual, kern_ref[...], noise_ref[:, 0:1])
-    new_ref[...] = own_piece(part_all(correction))
-    whole = correction.astype(BF16)
-    for to in range(N_X):
-        msg_ref[to] = whole
+    mine = own_piece([near_ref[i] for i in range(N_X * N_C)])
+    mine_ref[...] = own_ref[...] - by_half(damping) * mine
 
 
 def last_sums_body(recv_ref, corr_ref, noise_ref, mine_ref, msg_ref, applied_ref):
@@ -317,9 +305,9 @@
 def body(features, targets, point_order, lengthscale, noise_var):
     packed = (RHS // 2, 2 * OWN)
     n_p = N_X * N_C
-    plane_msg, noise = call(
+    plane_msg, feat_msg, noise = call(
         pack_body,
-        [((n_p, 32, 128), F32), ((RHS, 128), F32)],
+        [((n_p, 32, 128), F32), ((N_Z, 8, 128), F32), ((RHS, 128), F32)],
         *map(stay, (features, targets, point_order[None, :], lengthscale, noise_var)),
         scratch=[
             pltpu.VMEM((FEATS, OWN), F32),
@@ -333,60 +321,65 @@
         name="pack",
     )
     plane = swap(plane_msg, PLANE)
-    line_msg, kern_b, res, corr = call(
+    feat = swap(feat_msg, Z)
+    blocks, state, corr, own, left = call(
         first_body,
         [
-            ((N_Z, 40, 128), BF16),
-            ((BLOCK, BLOCK), BF16),
-            ((RHS, BLOCK), F32),
+            ((N_X, BLOCK, BLOCK), BF16),
+            ((2 * RHS, FLAT), F32),
             (packed, F32),
+            (packed, F32),
+            ((FLAT, DEPTH), BF16),
         ],
         plane,
         noise,
+        flops=1 << 31,
         name="first",
     )
+    line_msg, kern = call(
+        build_body,
+        [((N_Z, *packed), F32), ((FLAT, LINE), BF16)],
+        feat,
+        left,
+        state,
+        name="build",
+    )
     line = swap(line_msg, Z)
-    flat_msg, kern = call(
-        build_body,
-        [((n_p, *packed), F32), ((LINE, FLAT), BF16)],
-        line,
-        plane,
-        scratch=[pltpu.VMEM((DEPTH, LINE), BF16), pltpu.VMEM((DEPTH, FLAT), BF16)],
-        name="build",
-    )
-    flat = swap(flat_msg, PLANE)
     (share_msg,) = call(
-        share_body, [((N_C, *packed), F32)], flat, corr, noise, name="share"
-    )
-    shared = swap(share_msg, COLS)
-    (sums_msg,) = call(sums_body, [((N_X * N_Z, 128), F32)], shared, res, name="sums")
-    sums = swap(sums_msg, ROWS)
-    near_x_msg, corr_2, sol, mine = call(
+        share_body, [((n_p, *packed), F32)], line, corr, noise, name="share"
+    )
+    shared = swap(share_msg, PLANE)
+    sums_msg, applied = call(
+        sums_body, [((N_Z, 128), F32), ((RHS, FLAT), F32)], shared, state, name="sums"
+    )
+    sums = swap(sums_msg, Z)
+    line_msg, corr_2, sol, mine = call(
         second_body,
-        [((N_X, RHS, BLOCK), BF16), (packed, F32), (packed, F32), (packed, F32)],
+        [((N_Z, *packed), F32), (packed, F32), (packed, F32), (packed, F32)],
         sums,
+        applied,
+        state,
+        blocks,
+        kern,
+        noise,
+        corr,
+        own,
         shared,
-        res,
-        corr,
-        kern_b,
-        noise,
         name="second",
     )
-    near_x = swap(near_x_msg, X)
-    (line_msg,) = call(apply_body, [((N_Z, *packed), F32)], near_x, kern, name="apply")
-    flat = swap(line_msg, Z)
+    line = swap(line_msg, Z)
     near_msg, applied = call(
         last_sums_body,
-        [((N_C, 128), F32), (packed, F32)],
-        flat,
+        [((n_p, 128), F32), (packed, F32)],
+        line,
         corr_2,
         noise,
         mine,
         name="last_sums",
     )
-    near = swap(near_msg, COLS)
-    (sums_msg,) = call(gather_body, [((N_X * N_Z, 128), F32)], near, name="near")
-    sums = swap(sums_msg, ROWS)
+    near = swap(near_msg, PLANE)
+    (sums_msg,) = call(gather_body, [((N_Z, 128), F32)], near, name="near")
+    sums = swap(sums_msg, Z)
     return tuple(
         call(
             end_body,

time: 155 us -> 149 us (0.961)
  blocking collectives: 141 us -> 113 us
  starting transfers between devices: 0 us -> 13.1 us
  waiting for transfers between devices: 0 us -> 5.64 us
  Pallas kernels: 12.6 us -> 15.2 us
    all_to_all x9 -> x7, blocking collectives: 141 us -> 113 us  [swap(): return lax.all_to_all(array, axis, split_axis=0, concat_axis=0, tiled=True)]
    all_to_all x0 -> x1, starting transfers between devices: none -> 13.1 us  [swap(): return lax.all_to_all(array, axis, split_axis=0, concat_axis=0, tiled=True)]
    all_to_all x0 -> x1, waiting for transfers between devices: none -> 5.64 us  [swap(): return lax.all_to_all(array, axis, split_axis=0, concat_axis=0, tiled=True)]
    pallas_call x10 -> x9, Pallas kernels: 12.6 us -> 15.2 us  [call(): pl.pallas_call(body, out_shape=[jax.ShapeDtypeStruct(s, d) for s, d in ou...]
  transfers between devices with their start and end apart: 0 -> 1, of which waited for: 0 -> 1; matrix products, arithmetic and copies ran while one was open for 0% -> 0% of each run, Pallas kernels for 0% -> 3%
where the time goes in v3:
time: 149 us
  blocking collectives  113 us (76%)
  Pallas kernels  15.2 us (10%)
  starting transfers between devices  13.1 us (9%)
  waiting for transfers between devices  5.64 us (4%)
    all_to_all x7, blocking collectives, swap(): return lax.all_to_all(array, axis, split_axis=0, concat_axis=0, tiled=True)  113 us
    pallas_call x9, Pallas kernels, call(): pl.pallas_call(body, out_shape=[jax.ShapeDtypeStruct(s, d) for s, d in ou...  15.2 us
    all_to_all x1, starting transfers between devices, swap(): return lax.all_to_all(array, axis, split_axis=0, concat_axis=0, tiled=True)  13.1 us
    all_to_all x1, waiting for transfers between devices, swap(): return lax.all_to_all(array, axis, split_axis=0, concat_axis=0, tiled=True)  5.64 us
  transfers between devices with their start and end apart: 1, of which 1 were waited for; matrix products, arithmetic and copies ran while one was open for 0% of the time, Pallas kernels for 3%

profile of v3, /device:TPU:1, one launch (start us, length us, event | category | flops | bytes accessed | tf_op | source)
XLA Modules:
  0.0 148.6 jit_solution(14009786997908071644)
XLA Ops:
  0.6 1.5 %pack.1 = (f32[32,32,128]{2,1,0:T(8,128)S(1)}, f32[16,8,128]{2,1,0:T(8,128)}, f32[32,128]{1,0:T(8,128)S(1)}) custom-call(f32[16,64]{1,0:T(8,128)} %feat_any.1, f32[32,64]{1,0:T(8,128)} %targ_any.1, s32[1,64]{1,0:T(1,128)} %bitcast.19, f32[16]{0:T(128)} %scale_any.1, f32[32]{0:T(128)} %noise_any.1), custom_call_target="tpu_custom_call" | custom-call | flops 1048576 | bytes 1048576 | tf_op jit(solution)/shard_map/pack/pallas_call | solution.py:285
  2.2 21.9 %all_to_all.58.recv_ref = f32[32,32,128]{2,1,0:T(8,128)} all-to-all(f32[32,32,128]{2,1,0:T(8,128)S(1)} %get-tuple-element.21), channel_id=1, replica_groups=mesh['rows_0'=4,'rows_1'=16,'cols_0'=4,'cols_1'=2] {'rows_0','cols_0','c..., dimensions={0} | all-to-all | bytes 1048576 | tf_op jit(solution)/shard_map/all_to_all | solution.py:302
  24.0 13.1 %all-to-all-start = ((f32[16,8,128]{2,1,0:T(8,128)}), f32[16,8,128]{2,1,0:T(8,128)S(1)}, u32[]{:S(2)}, u32[]{:S(2)}) async-start(f32[16,8,128]{2,1,0:T(8,128)} %get-tuple-element.20), calls=%async_computation | async-start | bytes 131072 | tf_op jit(solution)/shard_map/all_to_all | solution.py:302
  37.2 0.0 copy-start
  37.2 1.0 copy-done
  38.2 5.0 %first.1 = (bf16[4,512,512]{2,1,0:T(8,128)(2,1)S(1)}, f32[64,2048]{1,0:T(8,128)S(1)}, f32[16,128]{1,0:T(8,128)S(1)}, f32[16,128]{1,0:T(8,128)S(1)}, bf16[2048,112]{1,0:T(8,128)(2,1)S(1)}) custom-call(f32[32,32,128]{2,1,0:T(8,128)S(1)} %copy-done, f32[32,128]{1,0:T(8,128)S(1)} %get-tuple-element.22.noise_ref), custom_call_target="tpu_custom_call" | custom-call | flops 2147483648 | bytes 1048576 | tf_op jit(solution)/shard_map/first/pallas_call | solution.py:285
  43.2 5.6 %all-to-all-done.line_ref = f32[16,8,128]{2,1,0:T(8,128)S(1)} async-done(((f32[16,8,128]{2,1,0:T(8,128)}), f32[16,8,128]{2,1,0:T(8,128)S(1)}, u32[]{:S(2)}, u32[]{:S(2)}) %all-to-all-start) | async-done | bytes 65568 | tf_op jit(solution)/shard_map/all_to_all | solution.py:302
  48.8 3.0 %build.1 = (f32[16,16,128]{2,1,0:T(8,128)S(1)}, bf16[2048,1024]{1,0:T(8,128)(2,1)S(1)}) custom-call(f32[16,8,128]{2,1,0:T(8,128)S(1)} %all-to-all-done.line_ref, bf16[2048,112]{1,0:T(8,128)(2,1)S(1)} %get-tuple-element.23.left_ref, f32[64,2048]{1,0:T(8,128)S(1)} %get-tuple-element.24.state_ref.res_ref), custom_call_target="tpu_custom_call" | custom-call | flops 1048576 | bytes 1048576 | tf_op jit(solution)/shard_map/build/pallas_call | solution.py:285
  51.8 17.7 %all_to_all.59.recv_ref = f32[16,16,128]{2,1,0:T(8,128)S(1)} all-to-all(f32[16,16,128]{2,1,0:T(8,128)S(1)} %get-tuple-element.25), channel_id=1, replica_groups=mesh['rows_0'=4,'rows_1'=16,'cols_0'=4,'cols_1'=2] {'rows_1'}, dimensions={0} | all-to-all | bytes 262144 | tf_op jit(solution)/shard_map/all_to_all | solution.py:302
  69.6 0.1 share.1
  69.7 15.5 %all_to_all.60.recv_ref.near_ref = f32[32,16,128]{2,1,0:T(8,128)S(1)} all-to-all(f32[32,16,128]{2,1,0:T(8,128)S(1)} %share.1), channel_id=1, replica_groups=mesh['rows_0'=4,'rows_1'=16,'cols_0'=4,'cols_1'=2] {'rows_0','cols_0','c..., dimensions={0} | all-to-all | bytes 524288 | tf_op jit(solution)/shard_map/all_to_all | solution.py:302
  85.1 0.3 sums.1
  85.5 14.9 %all_to_all.61 = f32[16,1,128]{2,1,0:T(1,128)S(1)} all-to-all(f32[16,1,128]{2,1,0:T(1,128)S(1)} %bitcast.18), channel_id=1, replica_groups=mesh['rows_0'=4,'rows_1'=16,'cols_0'=4,'cols_1'=2] {'rows_1'}, dimensions={0} | all-to-all | bytes 16384 | tf_op jit(solution)/shard_map/all_to_all | solution.py:302
  100.4 4.1 %second.1 = (f32[16,16,128]{2,1,0:T(8,128)S(1)}, f32[16,128]{1,0:T(8,128)S(1)}, f32[16,128]{1,0:T(8,128)S(1)}, f32[16,128]{1,0:T(8,128)S(1)}) custom-call(f32[16,128]{1,0:T(8,128)S(1)} %bitcast.16, f32[32,2048]{1,0:T(8,128)S(1)} %get-tuple-element.28.applied_ref, f32[64,2048]{1,0:T(8,128)S(1)} %get-tuple-element.24.state_ref.res_ref, ...), custom_call_target="tpu_custom_call" | custom-call | flops 1048576 | bytes 1048576 | tf_op jit(solution)/shard_map/second/pallas_call | solution.py:285
  104.4 14.5 %all_to_all.62.recv_ref = f32[16,16,128]{2,1,0:T(8,128)S(1)} all-to-all(f32[16,16,128]{2,1,0:T(8,128)S(1)} %get-tuple-element.32), channel_id=1, replica_groups=mesh['rows_0'=4,'rows_1'=16,'cols_0'=4,'cols_1'=2] {'rows_1'}, dimensions={0} | all-to-all | bytes 262144 | tf_op jit(solution)/shard_map/all_to_all | solution.py:302
  119.0 0.3 last_sums.1
  119.3 13.7 %all_to_all.63 = f32[32,1,128]{2,1,0:T(1,128)S(1)} all-to-all(f32[32,1,128]{2,1,0:T(1,128)S(1)} %bitcast.17), channel_id=1, replica_groups=mesh['rows_0'=4,'rows_1'=16,'cols_0'=4,'cols_1'=2] {'rows_0','cols_0','c..., dimensions={0} | all-to-all | bytes 32768 | tf_op jit(solution)/shard_map/all_to_all | solution.py:302
  133.1 14.7 %all_to_all.64 = f32[16,1,128]{2,1,0:T(1,128)S(1)} all-to-all(f32[16,1,128]{2,1,0:T(1,128)S(1)} %bitcast.15), channel_id=1, replica_groups=mesh['rows_0'=4,'rows_1'=16,'cols_0'=4,'cols_1'=2] {'rows_1'}, dimensions={0} | all-to-all | bytes 16384 | tf_op jit(solution)/shard_map/all_to_all | solution.py:302
  147.7 0.8 end.1
  (1 shorter events, 0.0 us)
Async XLA Ops:
  24.0 24.8 %all-to-all-start = ((f32[16,8,128]{2,1,0:T(8,128)}), f32[16,8,128]{2,1,0:T(8,128)S(1)}, u32[]{:S(2)}, u32[]{:S(2)}) async-start(f32[16,8,128]{2,1,0:T(8,128)} %get-tuple-element.20), calls=%async_computation | async-start | bytes 131072 | tf_op jit(solution)/shard_map/all_to_all | solution.py:302
  37.2 1.0 copy-start

commit v4 on v3

--- a/solution.py
+++ b/solution.py
@@ -85,21 +85,35 @@
     return jnp.concatenate([*order, tail], axis=0).astype(BF16)
 
 
-def block_cg(residual, kern, noise):
-    remains, direction = residual, residual
-    correction = jnp.zeros_like(residual)
+def plane_cg(residual, kern_ref, noise):
+    def stack(field):
+        return jnp.concatenate([cut(field, x) for x in range(N_X)], axis=0)
+
+    def image_of(direction):
+        packed = direction.astype(BF16)
+        images = [
+            jnp.dot(
+                packed[x * RHS : (x + 1) * RHS], kern_ref[x], preferred_element_type=F32
+            )
+            for x in range(N_X)
+        ]
+        return jnp.concatenate(images, axis=0) + shift * direction
+
+    shift = jnp.concatenate([noise] * N_X, axis=0)
+    remains = direction = stack(residual)
+    correction = jnp.zeros_like(remains)
     res_norm = jnp.sum(remains * remains, axis=1, keepdims=True)
     for turn in range(INNER):
-        image = jnp.dot(direction.astype(BF16), kern, preferred_element_type=F32)
-        image = image + noise * direction
+        image = image_of(direction)
         step = res_norm / jnp.sum(direction * image, axis=1, keepdims=True)
         correction = correction + step * direction
-        remains = remains - step * image
         if turn + 1 < INNER:
+            remains = remains - step * image
             new_norm = jnp.sum(remains * remains, axis=1, keepdims=True)
             direction = remains + (new_norm / res_norm) * direction
             res_norm = new_norm
-    return correction
+    pieces = [correction[x * RHS : (x + 1) * RHS] for x in range(N_X)]
+    return jnp.concatenate(pieces, axis=1)
 
 
 def sums_row(residual, applied):
@@ -155,8 +169,7 @@
     whole = jnp.concatenate([scaled, halves(targ_ref[...]), order], axis=0)
     for to in range(N_X * N_C):
         plane_ref[to] = whole
-    for to in range(N_Z):
-        line_ref[to] = scaled
+    line_ref[...] = scaled
     noise_ref[...] = column(given_ref, (RHS, 128))
 
 
@@ -167,8 +180,6 @@
 def first_body(
     recv_ref, noise_ref, kern_ref, state_ref, mine_ref, own_ref, left_ref
 ):
-    mine = []
-    residuals = []
     for x in range(N_X):
         pieces = [recv_ref[x * N_C + i] for i in range(N_C)]
         parts = three(join_all([p[0:8] for p in pieces]))
@@ -189,12 +200,11 @@
         moved = jnp.dot(stack, pick, preferred_element_type=F32)
         residual = moved[0:RHS] + (moved[RHS : 2 * RHS] + moved[2 * RHS :])
         state_ref[0:RHS, pl.ds(x * BLOCK, BLOCK)] = residual
-        correction = block_cg(residual, kern_ref[x], noise_ref[:, 0:1])
-        state_ref[RHS:, pl.ds(x * BLOCK, BLOCK)] = correction
-        mine += part_all(correction)
-        residuals += part_all(residual)
-    mine_ref[...] = own_piece(mine)
-    own_ref[...] = own_piece(residuals)
+    residual = state_ref[0:RHS, :]
+    correction = plane_cg(residual, kern_ref, noise_ref[:, 0:1])
+    state_ref[RHS:, :] = correction
+    mine_ref[...] = own_piece(part_all(correction))
+    own_ref[...] = own_piece(part_all(residual))
 
 
 def spread(msg_ref, at, field):
@@ -206,10 +216,13 @@
 
 
 def build_body(line_ref, left_ref, state_ref, msg_ref, kern_ref):
+    def piece(i):
+        return line_ref[pl.ds(8 * i, 8), :]
+
     packed = state_ref[RHS:, :].astype(BF16)
     for at in range(0, LINE, TILE):
         tiles = range(at // OWN, (at + TILE) // OWN, 2)
-        field = jnp.concatenate([join(line_ref[i], line_ref[i + 1]) for i in tiles], axis=1)
+        field = jnp.concatenate([join(piece(i), piece(i + 1)) for i in tiles], axis=1)
         exponent = jnp.dot(
             left_ref[...], factors(three(field), 1), preferred_element_type=F32
         )
@@ -245,10 +258,7 @@
 ):
     damping = damping_of(rows_ref[...])
     residual = res_ref[0:RHS, :] - damping * applied_ref[...]
-    corrections = [
-        block_cg(cut(residual, x), block_ref[x], noise_ref[:, 0:1]) for x in range(N_X)
-    ]
-    correction = jnp.concatenate(corrections, axis=1)
+    correction = plane_cg(residual, block_ref, noise_ref[:, 0:1])
     packed = correction.astype(BF16)
     for at in range(0, LINE, TILE):
         moved = jnp.dot(packed, kern_ref[:, pl.ds(at, TILE)], preferred_element_type=F32)
@@ -307,7 +317,7 @@
     n_p = N_X * N_C
     plane_msg, feat_msg, noise = call(
         pack_body,
-        [((n_p, 32, 128), F32), ((N_Z, 8, 128), F32), ((RHS, 128), F32)],
+        [((n_p, 32, 128), F32), ((8, 128), F32), ((RHS, 128), F32)],
         *map(stay, (features, targets, point_order[None, :], lengthscale, noise_var)),
         scratch=[
             pltpu.VMEM((FEATS, OWN), F32),
@@ -321,7 +331,7 @@
         name="pack",
     )
     plane = swap(plane_msg, PLANE)
-    feat = swap(feat_msg, Z)
+    feat = lax.all_gather(feat_msg, Z, axis=0, tiled=True)
     blocks, state, corr, own, left = call(
         first_body,
         [

time: 149 us -> 150 us (level)
  blocking collectives: 113 us -> 128 us
  waiting for transfers between devices: 5.64 us -> 0.01 us
  Pallas kernels: 15.2 us -> 11.4 us
  starting transfers between devices: 13.1 us -> 10.4 us
    all_gather x0 -> x1, blocking collectives: none -> 27.4 us  [body(): feat = lax.all_gather(feat_msg, Z, axis=0, tiled=True)]
    all_to_all x7 -> x6, blocking collectives: 113 us -> 100 us  [swap(): return lax.all_to_all(array, axis, split_axis=0, concat_axis=0, tiled=True)]
    all_to_all x1, waiting for transfers between devices: 5.64 us -> 0.01 us  [swap(): return lax.all_to_all(array, axis, split_axis=0, concat_axis=0, tiled=True)]
    pallas_call x9, Pallas kernels: 15.2 us -> 11.4 us  [call(): pl.pallas_call(body, out_shape=[jax.ShapeDtypeStruct(s, d) for s, d in ou...]
    all_to_all x1, starting transfers between devices: 13.1 us -> 10.4 us  [swap(): return lax.all_to_all(array, axis, split_axis=0, concat_axis=0, tiled=True)]
  transfers between devices with their start and end apart: 1 -> 1, of which waited for: 1 -> 0; matrix products, arithmetic and copies ran while one was open for 0% -> 0% of each run, Pallas kernels for 3% -> 0%
where the time goes in v4:
time: 150 us
  blocking collectives  128 us (85%)
  Pallas kernels  11.4 us (8%)
  starting transfers between devices  10.4 us (7%)
    all_to_all x6, blocking collectives, swap(): return lax.all_to_all(array, axis, split_axis=0, concat_axis=0, tiled=True)  100 us
    all_gather x1, blocking collectives, body(): feat = lax.all_gather(feat_msg, Z, axis=0, tiled=True)  27.4 us
    pallas_call x9, Pallas kernels, call(): pl.pallas_call(body, out_shape=[jax.ShapeDtypeStruct(s, d) for s, d in ou...  11.4 us
    all_to_all x1, starting transfers between devices, swap(): return lax.all_to_all(array, axis, split_axis=0, concat_axis=0, tiled=True)  10.4 us
  transfers between devices with their start and end apart: 1, of which 0 were waited for; matrix products, arithmetic and copies ran while one was open for 0% of the time, Pallas kernels for 0%

profile of v4, /device:TPU:1, one launch (start us, length us, event | category | flops | bytes accessed | tf_op | source)
XLA Modules:
  0.0 150.0 jit_solution(9926524953952982342)
XLA Ops:
  0.6 1.7 %pack.1 = (f32[32,32,128]{2,1,0:T(8,128)}, f32[8,128]{1,0:T(8,128)S(1)}, f32[32,128]{1,0:T(8,128)S(1)}) custom-call(f32[16,64]{1,0:T(8,128)} %feat_any.1, f32[32,64]{1,0:T(8,128)} %targ_any.1, s32[1,64]{1,0:T(1,128)} %bitcast.19, f32[16]{0:T(128)} %scale_any.1, f32[32]{0:T(128)} %noise_any.1), custom_call_target="tpu_custom_call" | custom-call | flops 1048576 | bytes 1048576 | tf_op jit(solution)/shard_map/pack/pallas_call | solution.py:295
  2.3 10.4 %all-to-all-start = ((f32[32,32,128]{2,1,0:T(8,128)}), f32[32,32,128]{2,1,0:T(8,128)S(1)}, u32[]{:S(2)}, u32[]{:S(2)}) async-start(f32[32,32,128]{2,1,0:T(8,128)} %get-tuple-element.21), calls=%async_computation | async-start | bytes 1048576 | tf_op jit(solution)/shard_map/all_to_all | solution.py:312
  12.7 27.4 %all_gather.3.line_ref = f32[128,128]{1,0:T(8,128)S(1)} all-gather(f32[8,128]{1,0:T(8,128)S(1)} %get-tuple-element.20), channel_id=1, replica_groups=mesh['rows_0'=4,'rows_1'=16,'cols_0'=4,'cols_1'=2] {'rows_1'}, dimensions={0}, use_global_device_ids=true | all-gather | bytes 69632 | tf_op jit(solution)/shard_map/all_gather | solution.py:334
  40.1 0.0 all-to-all-done.recv_ref
  40.1 2.8 %first.1 = (bf16[4,512,512]{2,1,0:T(8,128)(2,1)S(1)}, f32[64,2048]{1,0:T(8,128)S(1)}, f32[16,128]{1,0:T(8,128)S(1)}, f32[16,128]{1,0:T(8,128)S(1)}, bf16[2048,112]{1,0:T(8,128)(2,1)S(1)}) custom-call(f32[32,32,128]{2,1,0:T(8,128)S(1)} %all-to-all-done.recv_ref, f32[32,128]{1,0:T(8,128)S(1)} %get-tuple-element.22.noise_ref), custom_call_target="tpu_custom_call" | custom-call | flops 2147483648 | bytes 1048576 | tf_op jit(solution)/shard_map/first/pallas_call | solution.py:295
  42.9 3.0 %build.1 = (f32[16,16,128]{2,1,0:T(8,128)S(1)}, bf16[2048,1024]{1,0:T(8,128)(2,1)S(1)}) custom-call(f32[128,128]{1,0:T(8,128)S(1)} %all_gather.3.line_ref, bf16[2048,112]{1,0:T(8,128)(2,1)S(1)} %get-tuple-element.23.left_ref, f32[64,2048]{1,0:T(8,128)S(1)} %get-tuple-element.24.state_ref.res_ref), custom_call_target="tpu_custom_call" | custom-call | flops 1048576 | bytes 1048576 | tf_op jit(solution)/shard_map/build/pallas_call | solution.py:295
  45.9 18.6 %all_to_all.53.recv_ref = f32[16,16,128]{2,1,0:T(8,128)S(1)} all-to-all(f32[16,16,128]{2,1,0:T(8,128)S(1)} %get-tuple-element.25), channel_id=1, replica_groups=mesh['rows_0'=4,'rows_1'=16,'cols_0'=4,'cols_1'=2] {'rows_1'}, dimensions={0} | all-to-all | bytes 262144 | tf_op jit(solution)/shard_map/all_to_all | solution.py:312
  64.5 0.1 share.1
  64.6 23.8 %all_to_all.54.recv_ref.near_ref = f32[32,16,128]{2,1,0:T(8,128)S(1)} all-to-all(f32[32,16,128]{2,1,0:T(8,128)S(1)} %share.1), channel_id=1, replica_groups=mesh['rows_0'=4,'rows_1'=16,'cols_0'=4,'cols_1'=2] {'rows_0','cols_0','c..., dimensions={0} | all-to-all | bytes 524288 | tf_op jit(solution)/shard_map/all_to_all | solution.py:312
  88.4 0.3 sums.1
  88.7 14.8 %all_to_all.55 = f32[16,1,128]{2,1,0:T(1,128)S(1)} all-to-all(f32[16,1,128]{2,1,0:T(1,128)S(1)} %bitcast.18), channel_id=1, replica_groups=mesh['rows_0'=4,'rows_1'=16,'cols_0'=4,'cols_1'=2] {'rows_1'}, dimensions={0} | all-to-all | bytes 16384 | tf_op jit(solution)/shard_map/all_to_all | solution.py:312
  103.6 2.3 %second.1 = (f32[16,16,128]{2,1,0:T(8,128)S(1)}, f32[16,128]{1,0:T(8,128)S(1)}, f32[16,128]{1,0:T(8,128)S(1)}, f32[16,128]{1,0:T(8,128)S(1)}) custom-call(f32[16,128]{1,0:T(8,128)S(1)} %bitcast.16, f32[32,2048]{1,0:T(8,128)S(1)} %get-tuple-element.28.applied_ref, f32[64,2048]{1,0:T(8,128)S(1)} %get-tuple-element.24.state_ref.res_ref, ...), custom_call_target="tpu_custom_call" | custom-call | flops 1048576 | bytes 1048576 | tf_op jit(solution)/shard_map/second/pallas_call | solution.py:295
  105.8 14.5 %all_to_all.56.recv_ref = f32[16,16,128]{2,1,0:T(8,128)S(1)} all-to-all(f32[16,16,128]{2,1,0:T(8,128)S(1)} %get-tuple-element.32), channel_id=1, replica_groups=mesh['rows_0'=4,'rows_1'=16,'cols_0'=4,'cols_1'=2] {'rows_1'}, dimensions={0} | all-to-all | bytes 262144 | tf_op jit(solution)/shard_map/all_to_all | solution.py:312
  120.4 0.3 last_sums.1
  120.7 13.7 %all_to_all.57 = f32[32,1,128]{2,1,0:T(1,128)S(1)} all-to-all(f32[32,1,128]{2,1,0:T(1,128)S(1)} %bitcast.17), channel_id=1, replica_groups=mesh['rows_0'=4,'rows_1'=16,'cols_0'=4,'cols_1'=2] {'rows_0','cols_0','c..., dimensions={0} | all-to-all | bytes 32768 | tf_op jit(solution)/shard_map/all_to_all | solution.py:312
  134.4 14.7 %all_to_all.58 = f32[16,1,128]{2,1,0:T(1,128)S(1)} all-to-all(f32[16,1,128]{2,1,0:T(1,128)S(1)} %bitcast.15), channel_id=1, replica_groups=mesh['rows_0'=4,'rows_1'=16,'cols_0'=4,'cols_1'=2] {'rows_1'}, dimensions={0} | all-to-all | bytes 16384 | tf_op jit(solution)/shard_map/all_to_all | solution.py:312
  149.1 0.8 end.1
  (1 shorter events, 0.0 us)
Async XLA Ops:
  2.3 37.8 %all-to-all-start = ((f32[32,32,128]{2,1,0:T(8,128)}), f32[32,32,128]{2,1,0:T(8,128)S(1)}, u32[]{:S(2)}, u32[]{:S(2)}) async-start(f32[32,32,128]{2,1,0:T(8,128)} %get-tuple-element.21), calls=%async_computation | async-start | bytes 1048576 | tf_op jit(solution)/shard_map/all_to_all | solution.py:312

commit v5 on v4

--- a/solution.py
+++ b/solution.py
@@ -8,12 +8,13 @@
 
 INNER = 3
 X, Z, Y, K = "rows_0", "rows_1", "cols_0", "cols_1"
-PLANE = (X, Y, K)
+ROWS, COLS, PLANE = (X, Z), (Y, K), (X, Y, K)
 ROWS_COLS = (X, Z, Y, K)
 N_X, N_Z, N_C = 4, 16, 8
 FEATS, RHS, OWN, BLOCK = 16, 32, 64, 512
 LINE, FLAT = N_Z * OWN, N_X * BLOCK
 DEPTH = 7 * FEATS
+SENT = FEATS // 2 + RHS // 2 + 1
 ROOT_LOG2E = 1.4426950408889634**0.5
 F32, BF16 = jnp.float32, jnp.bfloat16
 PARAMS = pltpu.CompilerParams(vmem_limit_bytes=12 * 1024 * 1024)
@@ -131,14 +132,36 @@
     return turned[0:RHS, 0:1] / (turned[RHS : 2 * RHS, 0:1] + 1e-6)
 
 
+def column(source, shape):
+    row = lax.broadcasted_iota(jnp.int32, shape, 0)
+    filled = jnp.zeros(shape, F32)
+    for i in range(shape[0]):
+        filled = jnp.where(row == i, source[i], filled)
+    return filled
+
+
+SIDE = pl.ds(FLAT, 128)
+
+
+def noise_of(state_ref):
+    return state_ref[0:RHS, FLAT : FLAT + 1]
+
+
+def own_correction(state_ref):
+    return state_ref[RHS : RHS + RHS // 2, SIDE]
+
+
+def own_residual(state_ref):
+    return state_ref[RHS + RHS // 2 :, SIDE]
+
+
 def pack_body(
-    feat_any, targ_any, order_any, scale_any, noise_any,
-    plane_ref, line_ref, noise_ref,
-    feat_ref, targ_ref, order_ref, scale_ref, given_ref, sems,
+    feat_any, targ_any, order_any, scale_any,
+    plane_ref, line_ref,
+    feat_ref, targ_ref, order_ref, scale_ref, sems,
 ):
     pairs = (
         (scale_any, scale_ref),
-        (noise_any, given_ref),
         (feat_any, feat_ref),
         (targ_any, targ_ref),
         (order_any, order_ref),
@@ -155,33 +178,26 @@
         half = field.shape[0] // 2
         return jnp.concatenate([field[:half], field[half:]], axis=1)
 
-    def column(source, shape):
-        row = lax.broadcasted_iota(jnp.int32, shape, 0)
-        filled = jnp.zeros(shape, F32)
-        for i in range(shape[0]):
-            filled = jnp.where(row == i, source[i], filled)
-        return filled
-
     scaled = halves(feat_ref[...] / column(scale_ref, (FEATS, OWN)) * ROOT_LOG2E)
     order = (order_ref[...] % BLOCK).astype(F32)
     order = jnp.concatenate([order, order], axis=1)
-    order = jnp.broadcast_to(order, (8, 2 * OWN))
     whole = jnp.concatenate([scaled, halves(targ_ref[...]), order], axis=0)
     for to in range(N_X * N_C):
-        plane_ref[to] = whole
-    line_ref[...] = scaled
-    noise_ref[...] = column(given_ref, (RHS, 128))
+        plane_ref[pl.ds(SENT * to, SENT), :] = whole
+    for to in range(N_Z):
+        line_ref[to] = scaled
 
 
 def cut(field, which):
     return field[:, which * BLOCK : (which + 1) * BLOCK]
 
 
-def first_body(
-    recv_ref, noise_ref, kern_ref, state_ref, mine_ref, own_ref, left_ref
-):
+def first_body(recv_ref, noise_any, kern_ref, state_ref, left_ref, given_ref, sem):
+    copy = pltpu.make_async_copy(noise_any, given_ref, sem)
+    copy.start()
     for x in range(N_X):
-        pieces = [recv_ref[x * N_C + i] for i in range(N_C)]
+        at = x * N_C * SENT
+        pieces = [recv_ref[pl.ds(at + i * SENT, SENT), :] for i in range(N_C)]
         parts = three(join_all([p[0:8] for p in pieces]))
         left = factors(parts, 0).T
         left_ref[pl.ds(x * BLOCK, BLOCK), :] = left
@@ -200,11 +216,14 @@
         moved = jnp.dot(stack, pick, preferred_element_type=F32)
         residual = moved[0:RHS] + (moved[RHS : 2 * RHS] + moved[2 * RHS :])
         state_ref[0:RHS, pl.ds(x * BLOCK, BLOCK)] = residual
-    residual = state_ref[0:RHS, :]
-    correction = plane_cg(residual, kern_ref, noise_ref[:, 0:1])
-    state_ref[RHS:, :] = correction
-    mine_ref[...] = own_piece(part_all(correction))
-    own_ref[...] = own_piece(part_all(residual))
+    copy.wait()
+    noise = column(given_ref, (RHS, 128))
+    state_ref[0:RHS, SIDE] = noise
+    residual = state_ref[0:RHS, 0:FLAT]
+    correction = plane_cg(residual, kern_ref, noise[:, 0:1])
+    state_ref[RHS:, 0:FLAT] = correction
+    both = [own_piece(part_all(field)) for field in (correction, residual)]
+    state_ref[RHS:, SIDE] = jnp.concatenate(both, axis=0)
 
 
 def spread(msg_ref, at, field):
@@ -217,9 +236,9 @@
 
 def build_body(line_ref, left_ref, state_ref, msg_ref, kern_ref):
     def piece(i):
-        return line_ref[pl.ds(8 * i, 8), :]
-
-    packed = state_ref[RHS:, :].astype(BF16)
+        return line_ref[i]
+
+    packed = state_ref[RHS:, 0:FLAT].astype(BF16)
     for at in range(0, LINE, TILE):
         tiles = range(at // OWN, (at + TILE) // OWN, 2)
         field = jnp.concatenate([join(piece(i), piece(i + 1)) for i in tiles], axis=1)
@@ -232,45 +251,45 @@
         spread(msg_ref, at // OWN, moved)
 
 
-def applied_of(recv_ref, corr_ref, noise_ref):
+def applied_of(recv_ref, correction, state_ref):
     total = recv_ref[0]
     for i in range(1, recv_ref.shape[0]):
         total = total + recv_ref[i]
-    return total + by_half(noise_ref[:, 0:1]) * corr_ref[...]
-
-
-def share_body(recv_ref, corr_ref, noise_ref, msg_ref):
-    applied = applied_of(recv_ref, corr_ref, noise_ref)
+    return total + by_half(noise_of(state_ref)) * correction
+
+
+def share_body(recv_ref, state_ref, msg_ref):
+    applied = applied_of(recv_ref, own_correction(state_ref), state_ref)
     for to in range(N_X * N_C):
         msg_ref[to] = applied
 
 
-def sums_body(recv_ref, res_ref, msg_ref, applied_ref):
+def sums_body(recv_ref, state_ref, msg_ref, applied_ref):
     applied = join_all([recv_ref[i] for i in range(N_X * N_C)])
     applied_ref[...] = applied
-    row = sums_row(res_ref[0:RHS, :], applied)
+    row = sums_row(state_ref[0:RHS, 0:FLAT], applied)
     msg_ref[...] = jnp.broadcast_to(row, msg_ref.shape)
 
 
 def second_body(
-    rows_ref, applied_ref, res_ref, block_ref, kern_ref, noise_ref, corr_ref, own_ref, near_ref,
+    rows_ref, applied_ref, state_ref, block_ref, kern_ref, near_ref,
     msg_ref, new_ref, sol_ref, mine_ref,
 ):
     damping = damping_of(rows_ref[...])
-    residual = res_ref[0:RHS, :] - damping * applied_ref[...]
-    correction = plane_cg(residual, block_ref, noise_ref[:, 0:1])
+    residual = state_ref[0:RHS, 0:FLAT] - damping * applied_ref[...]
+    correction = plane_cg(residual, block_ref, noise_of(state_ref))
     packed = correction.astype(BF16)
     for at in range(0, LINE, TILE):
         moved = jnp.dot(packed, kern_ref[:, pl.ds(at, TILE)], preferred_element_type=F32)
         spread(msg_ref, at // OWN, moved)
     new_ref[...] = own_piece(part_all(correction))
-    sol_ref[...] = by_half(damping) * corr_ref[...]
+    sol_ref[...] = by_half(damping) * own_correction(state_ref)
     mine = own_piece([near_ref[i] for i in range(N_X * N_C)])
-    mine_ref[...] = own_ref[...] - by_half(damping) * mine
-
-
-def last_sums_body(recv_ref, corr_ref, noise_ref, mine_ref, msg_ref, applied_ref):
-    applied = applied_of(recv_ref, corr_ref, noise_ref)
+    mine_ref[...] = own_residual(state_ref) - by_half(damping) * mine
+
+
+def last_sums_body(recv_ref, corr_ref, state_ref, mine_ref, msg_ref, applied_ref):
+    applied = applied_of(recv_ref, corr_ref[...], state_ref)
     applied_ref[...] = applied
     row = sums_row(split_halves(mine_ref[...]), split_halves(applied))
     msg_ref[...] = jnp.broadcast_to(row, msg_ref.shape)
@@ -291,11 +310,13 @@
     res_out[...] = split_halves(mine_ref[...] - damping * applied_ref[...])
 
 
-def call(body, outs, *args, scratch=(), space=pltpu.VMEM, flops=1 << 20, name):
+def call(body, outs, *args, scratch=(), spaces=None, flops=1 << 20, name):
     return pl.pallas_call(
         body,
         out_shape=[jax.ShapeDtypeStruct(s, d) for s, d in outs],
-        in_specs=[pl.BlockSpec(memory_space=space)] * len(args),
+        in_specs=[
+            pl.BlockSpec(memory_space=s) for s in spaces or (pltpu.VMEM,) * len(args)
+        ],
         out_specs=[pl.BlockSpec(memory_space=pltpu.VMEM)] * len(outs),
         scratch_shapes=list(scratch),
         compiler_params=PARAMS,
@@ -315,34 +336,33 @@
 def body(features, targets, point_order, lengthscale, noise_var):
     packed = (RHS // 2, 2 * OWN)
     n_p = N_X * N_C
-    plane_msg, feat_msg, noise = call(
+    plane_msg, feat_msg = call(
         pack_body,
-        [((n_p, 32, 128), F32), ((8, 128), F32), ((RHS, 128), F32)],
-        *map(stay, (features, targets, point_order[None, :], lengthscale, noise_var)),
+        [((n_p * SENT, 128), F32), ((N_Z, 8, 128), F32)],
+        *map(stay, (features, targets, point_order[None, :], lengthscale)),
         scratch=[
             pltpu.VMEM((FEATS, OWN), F32),
             pltpu.VMEM((RHS, OWN), F32),
             pltpu.VMEM((1, OWN), jnp.int32),
             pltpu.SMEM((FEATS,), F32),
-            pltpu.SMEM((RHS,), F32),
-            pltpu.SemaphoreType.DMA((5,)),
+            pltpu.SemaphoreType.DMA((4,)),
         ],
-        space=pltpu.HBM,
+        spaces=(pltpu.HBM,) * 4,
         name="pack",
     )
-    plane = swap(plane_msg, PLANE)
-    feat = lax.all_gather(feat_msg, Z, axis=0, tiled=True)
-    blocks, state, corr, own, left = call(
+    plane = swap(plane_msg.reshape(n_p, 1, SENT * 128), PLANE).reshape(n_p * SENT, 128)
+    feat = swap(feat_msg, Z)
+    blocks, state, left = call(
         first_body,
         [
             ((N_X, BLOCK, BLOCK), BF16),
-            ((2 * RHS, FLAT), F32),
-            (packed, F32),
-            (packed, F32),
+            ((2 * RHS, FLAT + 128), F32),
             ((FLAT, DEPTH), BF16),
         ],
         plane,
-        noise,
+        stay(noise_var),
+        scratch=[pltpu.SMEM((RHS,), F32), pltpu.SemaphoreType.DMA],
+        spaces=(pltpu.VMEM, pltpu.HBM),
         flops=1 << 31,
         name="first",
     )
@@ -356,7 +376,7 @@
     )
     line = swap(line_msg, Z)
     (share_msg,) = call(
-        share_body, [((n_p, *packed), F32)], line, corr, noise, name="share"
+        share_body, [((n_p, *packed), F32)], line, state, name="share"
     )
     shared = swap(share_msg, PLANE)
     sums_msg, applied = call(
@@ -371,25 +391,22 @@
         state,
         blocks,
         kern,
-        noise,
-        corr,
-        own,
         shared,
         name="second",
     )
     line = swap(line_msg, Z)
     near_msg, applied = call(
         last_sums_body,
-        [((n_p, 128), F32), (packed, F32)],
+        [((N_C, 128), F32), (packed, F32)],
         line,
         corr_2,
-        noise,
+        state,
         mine,
         name="last_sums",
     )
-    near = swap(near_msg, PLANE)
-    (sums_msg,) = call(gather_body, [((N_Z, 128), F32)], near, name="near")
-    sums = swap(sums_msg, Z)
+    near = swap(near_msg, COLS)
+    (sums_msg,) = call(gather_body, [((N_X * N_Z, 128), F32)], near, name="near")
+    sums = swap(sums_msg, ROWS)
     return tuple(
         call(
             end_body,

time: 150 us -> 145 us (0.967)
  blocking collectives: 128 us -> 111 us
  waiting for transfers between devices: 0.01 us -> 7.65 us
  starting transfers between devices: 10.4 us -> 13.1 us
    all_gather x1 -> x0, blocking collectives: 27.4 us -> none  [body(): feat = lax.all_gather(feat_msg, Z, axis=0, tiled=True)]
    all_to_all x6 -> x7, blocking collectives: 100 us -> 111 us  [swap(): return lax.all_to_all(array, axis, split_axis=0, concat_axis=0, tiled=True)]
    all_to_all x1, waiting for transfers between devices: 0.01 us -> 7.65 us  [swap(): return lax.all_to_all(array, axis, split_axis=0, concat_axis=0, tiled=True)]
    all_to_all x1, starting transfers between devices: 10.4 us -> 13.1 us  [swap(): return lax.all_to_all(array, axis, split_axis=0, concat_axis=0, tiled=True)]
  transfers between devices with their start and end apart: 1 -> 1, of which waited for: 0 -> 1; matrix products, arithmetic and copies ran while one was open for 0% -> 0% of each run, Pallas kernels for 0% -> 2%
where the time goes in v5:
time: 145 us; the launch traced here: 144 us
  blocking collectives  111 us (77%)
  starting transfers between devices  13.1 us (9%)
  Pallas kernels  11.3 us (8%)
  waiting for transfers between devices  7.65 us (5%)
    all_to_all x7, blocking collectives, swap(): return lax.all_to_all(array, axis, split_axis=0, concat_axis=0, tiled=True)  111 us
    all_to_all x1, starting transfers between devices, swap(): return lax.all_to_all(array, axis, split_axis=0, concat_axis=0, tiled=True)  13.1 us
    pallas_call x9, Pallas kernels, call(): pl.pallas_call(body, out_shape=[jax.ShapeDtypeStruct(s, d) for s, d in ou...  11.3 us
    all_to_all x1, waiting for transfers between devices, swap(): return lax.all_to_all(array, axis, split_axis=0, concat_axis=0, tiled=True)  7.65 us
  transfers between devices with their start and end apart: 1, of which 1 were waited for; matrix products, arithmetic and copies ran while one was open for 0% of the time, Pallas kernels for 2%

profile of v5, /device:TPU:1, one launch (start us, length us, event | category | flops | bytes accessed | tf_op | source)
XLA Modules:
  0.0 144.3 jit_solution(7691913516349133226)
XLA Ops:
  0.6 1.5 %pack.1 = (f32[800,128]{1,0:T(8,128)S(1)}, f32[16,8,128]{2,1,0:T(8,128)}) custom-call(f32[16,64]{1,0:T(8,128)} %feat_any.1, f32[32,64]{1,0:T(8,128)} %targ_any.1, s32[1,64]{1,0:T(1,128)} %bitcast.23, f32[16]{0:T(128)} %scale_any.1), custom_call_target="tpu_custom_call" | custom-call | flops 1048576 | bytes 1048576 | tf_op jit(solution)/shard_map/pack/pallas_call | solution.py:314
  2.1 20.7 %all_to_all.58 = f32[32,1,3200]{2,1,0:T(1,128)} all-to-all(f32[32,1,3200]{2,1,0:T(1,128)S(1)} %bitcast.16), channel_id=1, replica_groups=mesh['rows_0'=4,'rows_1'=16,'cols_0'=4,'cols_1'=2] {'rows_0','cols_0','c..., dimensions={0} | all-to-all | bytes 819200 | tf_op jit(solution)/shard_map/all_to_all | solution.py:333
  22.8 13.1 %all-to-all-start = ((f32[16,8,128]{2,1,0:T(8,128)}), f32[16,8,128]{2,1,0:T(8,128)S(1)}, u32[]{:S(2)}, u32[]{:S(2)}) async-start(f32[16,8,128]{2,1,0:T(8,128)} %get-tuple-element.17), calls=%async_computation | async-start | bytes 131072 | tf_op jit(solution)/shard_map/all_to_all | solution.py:333
  36.0 0.0 copy-start
  36.0 1.0 copy-done
  37.0 2.9 %first.1 = (bf16[4,512,512]{2,1,0:T(8,128)(2,1)S(1)}, f32[64,2176]{1,0:T(8,128)S(1)}, bf16[2048,112]{1,0:T(8,128)(2,1)S(1)}) custom-call(f32[800,128]{1,0:T(8,128)S(1)} %bitcast.15, f32[32]{0:T(128)} %noise_any.1), custom_call_target="tpu_custom_call" | custom-call | flops 2147483648 | bytes 1048576 | tf_op jit(solution)/shard_map/first/pallas_call | solution.py:314
  39.9 7.7 %all-to-all-done.line_ref = f32[16,8,128]{2,1,0:T(8,128)S(1)} async-done(((f32[16,8,128]{2,1,0:T(8,128)}), f32[16,8,128]{2,1,0:T(8,128)S(1)}, u32[]{:S(2)}, u32[]{:S(2)}) %all-to-all-start) | async-done | bytes 65568 | tf_op jit(solution)/shard_map/all_to_all | solution.py:333
  47.6 3.0 %build.1 = (f32[16,16,128]{2,1,0:T(8,128)S(1)}, bf16[2048,1024]{1,0:T(8,128)(2,1)S(1)}) custom-call(f32[16,8,128]{2,1,0:T(8,128)S(1)} %all-to-all-done.line_ref, bf16[2048,112]{1,0:T(8,128)(2,1)S(1)} %get-tuple-element.19.left_ref, f32[64,2176]{1,0:T(8,128)S(1)} %get-tuple-element.20.state_ref), custom_call_target="tpu_custom_call" | custom-call | flops 1048576 | bytes 1048576 | tf_op jit(solution)/shard_map/build/pallas_call | solution.py:314
  50.6 15.9 %all_to_all.59.recv_ref = f32[16,16,128]{2,1,0:T(8,128)S(1)} all-to-all(f32[16,16,128]{2,1,0:T(8,128)S(1)} %get-tuple-element.21), channel_id=1, replica_groups=mesh['rows_0'=4,'rows_1'=16,'cols_0'=4,'cols_1'=2] {'rows_1'}, dimensions={0} | all-to-all | bytes 262144 | tf_op jit(solution)/shard_map/all_to_all | solution.py:333
  66.4 0.1 share.1
  66.5 15.9 %all_to_all.60.recv_ref.near_ref = f32[32,16,128]{2,1,0:T(8,128)S(1)} all-to-all(f32[32,16,128]{2,1,0:T(8,128)S(1)} %share.1), channel_id=1, replica_groups=mesh['rows_0'=4,'rows_1'=16,'cols_0'=4,'cols_1'=2] {'rows_0','cols_0','c..., dimensions={0} | all-to-all | bytes 524288 | tf_op jit(solution)/shard_map/all_to_all | solution.py:333
  82.4 0.3 sums.1
  82.7 14.6 %all_to_all.61 = f32[16,1,128]{2,1,0:T(1,128)S(1)} all-to-all(f32[16,1,128]{2,1,0:T(1,128)S(1)} %bitcast.21), channel_id=1, replica_groups=mesh['rows_0'=4,'rows_1'=16,'cols_0'=4,'cols_1'=2] {'rows_1'}, dimensions={0} | all-to-all | bytes 16384 | tf_op jit(solution)/shard_map/all_to_all | solution.py:333
  97.3 2.3 %second.1 = (f32[16,16,128]{2,1,0:T(8,128)S(1)}, f32[16,128]{1,0:T(8,128)S(1)}, f32[16,128]{1,0:T(8,128)S(1)}, f32[16,128]{1,0:T(8,128)S(1)}) custom-call(f32[16,128]{1,0:T(8,128)S(1)} %bitcast.19, f32[32,2048]{1,0:T(8,128)S(1)} %get-tuple-element.23.applied_ref, f32[64,2176]{1,0:T(8,128)S(1)} %get-tuple-element.20.state_ref, ...), custom_call_target="tpu_custom_call" | custom-call | flops 1048576 | bytes 1048576 | tf_op jit(solution)/shard_map/second/pallas_call | solution.py:314
  99.6 14.5 %all_to_all.62.recv_ref = f32[16,16,128]{2,1,0:T(8,128)S(1)} all-to-all(f32[16,16,128]{2,1,0:T(8,128)S(1)} %get-tuple-element.26), channel_id=1, replica_groups=mesh['rows_0'=4,'rows_1'=16,'cols_0'=4,'cols_1'=2] {'rows_1'}, dimensions={0} | all-to-all | bytes 262144 | tf_op jit(solution)/shard_map/all_to_all | solution.py:333
  114.1 0.3 last_sums.1
  114.4 10.7 %all_to_all.63 = f32[8,1,128]{2,1,0:T(1,128)S(1)} all-to-all(f32[8,1,128]{2,1,0:T(1,128)S(1)} %bitcast.22), channel_id=1, replica_groups=mesh['rows_0'=4,'rows_1'=16,'cols_0'=4,'cols_1'=2] {'cols_0','cols_1'}, dimensions={0} | all-to-all | bytes 8192 | tf_op jit(solution)/shard_map/all_to_all | solution.py:333
  125.1 18.3 %all_to_all.64 = f32[64,1,128]{2,1,0:T(1,128)S(1)} all-to-all(f32[64,1,128]{2,1,0:T(1,128)S(1)} %bitcast.18), channel_id=1, replica_groups=mesh['rows_0'=4,'rows_1'=16,'cols_0'=4,'cols_1'=2] {'rows_0','rows_1'}, dimensions={0} | all-to-all | bytes 65536 | tf_op jit(solution)/shard_map/all_to_all | solution.py:333
  143.5 0.9 end.1
  (1 shorter events, 0.0 us)
Async XLA Ops:
  22.8 24.7 %all-to-all-start = ((f32[16,8,128]{2,1,0:T(8,128)}), f32[16,8,128]{2,1,0:T(8,128)S(1)}, u32[]{:S(2)}, u32[]{:S(2)}) async-start(f32[16,8,128]{2,1,0:T(8,128)} %get-tuple-element.17), calls=%async_computation | async-start | bytes 131072 | tf_op jit(solution)/shard_map/all_to_all | solution.py:333
  36.0 1.0 copy-start

commit v6 on v5

--- a/solution.py
+++ b/solution.py
@@ -8,13 +8,14 @@
 
 INNER = 3
 X, Z, Y, K = "rows_0", "rows_1", "cols_0", "cols_1"
-ROWS, COLS, PLANE = (X, Z), (Y, K), (X, Y, K)
+PLANE = (X, Y, K)
 ROWS_COLS = (X, Z, Y, K)
 N_X, N_Z, N_C = 4, 16, 8
 FEATS, RHS, OWN, BLOCK = 16, 32, 64, 512
 LINE, FLAT = N_Z * OWN, N_X * BLOCK
 DEPTH = 7 * FEATS
 SENT = FEATS // 2 + RHS // 2 + 1
+TILE = min(LINE, 256)
 ROOT_LOG2E = 1.4426950408889634**0.5
 F32, BF16 = jnp.float32, jnp.bfloat16
 PARAMS = pltpu.CompilerParams(vmem_limit_bytes=12 * 1024 * 1024)
@@ -86,7 +87,7 @@
     return jnp.concatenate([*order, tail], axis=0).astype(BF16)
 
 
-def plane_cg(residual, kern_ref, noise):
+def plane_cg(residual, kern_ref, noise, beside=None):
     def stack(field):
         return jnp.concatenate([cut(field, x) for x in range(N_X)], axis=0)
 
@@ -106,6 +107,8 @@
     res_norm = jnp.sum(remains * remains, axis=1, keepdims=True)
     for turn in range(INNER):
         image = image_of(direction)
+        if beside is not None:
+            beside(turn)
         step = res_norm / jnp.sum(direction * image, axis=1, keepdims=True)
         correction = correction + step * direction
         if turn + 1 < INNER:
@@ -192,9 +195,21 @@
     return field[:, which * BLOCK : (which + 1) * BLOCK]
 
 
-def first_body(recv_ref, noise_any, kern_ref, state_ref, left_ref, given_ref, sem):
+def first_body(
+    recv_ref, line_ref, noise_any, kern_ref, state_ref, tile_ref, msg_ref, left_ref, given_ref, sem
+):
     copy = pltpu.make_async_copy(noise_any, given_ref, sem)
     copy.start()
+    tiles = range(0, LINE, TILE)
+
+    def build(turn):
+        for at in tiles[turn :: INNER + 1]:
+            around = range(at // OWN, (at + TILE) // OWN, 2)
+            pairs = [join(line_ref[i], line_ref[i + 1]) for i in around]
+            right = factors(three(jnp.concatenate(pairs, axis=1)), 1)
+            exponent = jnp.dot(left_ref[...], right, preferred_element_type=F32)
+            tile_ref[:, pl.ds(at, TILE)] = jnp.exp2(exponent).astype(BF16)
+
     for x in range(N_X):
         at = x * N_C * SENT
         pieces = [recv_ref[pl.ds(at + i * SENT, SENT), :] for i in range(N_C)]
@@ -220,10 +235,12 @@
     noise = column(given_ref, (RHS, 128))
     state_ref[0:RHS, SIDE] = noise
     residual = state_ref[0:RHS, 0:FLAT]
-    correction = plane_cg(residual, kern_ref, noise[:, 0:1])
+    build(INNER)
+    correction = plane_cg(residual, kern_ref, noise[:, 0:1], build)
     state_ref[RHS:, 0:FLAT] = correction
     both = [own_piece(part_all(field)) for field in (correction, residual)]
     state_ref[RHS:, SIDE] = jnp.concatenate(both, axis=0)
+    apply(correction.astype(BF16), tile_ref, msg_ref)
 
 
 def spread(msg_ref, at, field):
@@ -231,23 +248,9 @@
         msg_ref[at + which] = piece
 
 
-TILE = min(LINE, 256)
-
-
-def build_body(line_ref, left_ref, state_ref, msg_ref, kern_ref):
-    def piece(i):
-        return line_ref[i]
-
-    packed = state_ref[RHS:, 0:FLAT].astype(BF16)
+def apply(packed, tile_ref, msg_ref):
     for at in range(0, LINE, TILE):
-        tiles = range(at // OWN, (at + TILE) // OWN, 2)
-        field = jnp.concatenate([join(piece(i), piece(i + 1)) for i in tiles], axis=1)
-        exponent = jnp.dot(
-            left_ref[...], factors(three(field), 1), preferred_element_type=F32
-        )
-        kern = jnp.exp2(exponent).astype(BF16)
-        kern_ref[:, pl.ds(at, TILE)] = kern
-        moved = jnp.dot(packed, kern, preferred_element_type=F32)
+        moved = jnp.dot(packed, tile_ref[:, pl.ds(at, TILE)], preferred_element_type=F32)
         spread(msg_ref, at // OWN, moved)
 
 
@@ -278,10 +281,7 @@
     damping = damping_of(rows_ref[...])
     residual = state_ref[0:RHS, 0:FLAT] - damping * applied_ref[...]
     correction = plane_cg(residual, block_ref, noise_of(state_ref))
-    packed = correction.astype(BF16)
-    for at in range(0, LINE, TILE):
-        moved = jnp.dot(packed, kern_ref[:, pl.ds(at, TILE)], preferred_element_type=F32)
-        spread(msg_ref, at // OWN, moved)
+    apply(correction.astype(BF16), kern_ref, msg_ref)
     new_ref[...] = own_piece(part_all(correction))
     sol_ref[...] = by_half(damping) * own_correction(state_ref)
     mine = own_piece([near_ref[i] for i in range(N_X * N_C)])
@@ -352,27 +352,24 @@
     )
     plane = swap(plane_msg.reshape(n_p, 1, SENT * 128), PLANE).reshape(n_p * SENT, 128)
     feat = swap(feat_msg, Z)
-    blocks, state, left = call(
+    blocks, state, kern, line_msg = call(
         first_body,
         [
             ((N_X, BLOCK, BLOCK), BF16),
             ((2 * RHS, FLAT + 128), F32),
-            ((FLAT, DEPTH), BF16),
+            ((FLAT, LINE), BF16),
+            ((N_Z, *packed), F32),
         ],
         plane,
+        feat,
         stay(noise_var),
-        scratch=[pltpu.SMEM((RHS,), F32), pltpu.SemaphoreType.DMA],
-        spaces=(pltpu.VMEM, pltpu.HBM),
-        flops=1 << 31,
+        scratch=[
+            pltpu.VMEM((FLAT, DEPTH), BF16),
+            pltpu.SMEM((RHS,), F32),
+            pltpu.SemaphoreType.DMA,
+        ],
+        spaces=(pltpu.VMEM, pltpu.VMEM, pltpu.HBM),
         name="first",
-    )
-    line_msg, kern = call(
-        build_body,
-        [((N_Z, *packed), F32), ((FLAT, LINE), BF16)],
-        feat,
-        left,
-        state,
-        name="build",
     )
     line = swap(line_msg, Z)
     (share_msg,) = call(
@@ -397,16 +394,16 @@
     line = swap(line_msg, Z)
     near_msg, applied = call(
         last_sums_body,
-        [((N_C, 128), F32), (packed, F32)],
+        [((n_p, 128), F32), (packed, F32)],
         line,
         corr_2,
         state,
         mine,
         name="last_sums",
     )
-    near = swap(near_msg, COLS)
-    (sums_msg,) = call(gather_body, [((N_X * N_Z, 128), F32)], near, name="near")
-    sums = swap(sums_msg, ROWS)
+    near = swap(near_msg, PLANE)
+    (sums_msg,) = call(gather_body, [((N_Z, 128), F32)], near, name="near")
+    sums = swap(sums_msg, Z)
     return tuple(
         call(
             end_body,

time: 145 us -> 144 us (level)
  blocking collectives: 111 us -> 134 us
  starting transfers between devices: 13.1 us -> 0 us
  waiting for transfers between devices: 7.65 us -> 0 us
  Pallas kernels: 11.3 us -> 8.87 us
    all_to_all x7 -> x8, blocking collectives: 111 us -> 134 us  [swap(): return lax.all_to_all(array, axis, split_axis=0, concat_axis=0, tiled=True)]
    all_to_all x1 -> x0, starting transfers between devices: 13.1 us -> none  [swap(): return lax.all_to_all(array, axis, split_axis=0, concat_axis=0, tiled=True)]
    all_to_all x1 -> x0, waiting for transfers between devices: 7.65 us -> none  [swap(): return lax.all_to_all(array, axis, split_axis=0, concat_axis=0, tiled=True)]
    pallas_call x9 -> x8, Pallas kernels: 11.3 us -> 8.87 us  [call(): pl.pallas_call(body, out_shape=[jax.ShapeDtypeStruct(s, d) for s, d in ou...]
  transfers between devices with their start and end apart: 1 -> 0, of which waited for: 1 -> 0; matrix products, arithmetic and copies ran while one was open for 0% -> 0% of each run, Pallas kernels for 2% -> 0%
where the time goes in v6:
time: 144 us
  blocking collectives  134 us (93%)
  Pallas kernels  8.87 us (6%)
    all_to_all x8, blocking collectives, swap(): return lax.all_to_all(array, axis, split_axis=0, concat_axis=0, tiled=True)  134 us
    pallas_call x8, Pallas kernels, call(): pl.pallas_call(body, out_shape=[jax.ShapeDtypeStruct(s, d) for s, d in ou...  8.87 us

profile of v6, /device:TPU:1, one launch (start us, length us, event | category | flops | bytes accessed | tf_op | source)
XLA Modules:
  0.0 144.0 jit_solution(9387420453770868942)
XLA Ops:
  0.6 0.9 pack.1
  1.5 27.1 %all_to_all.58.line_ref = f32[16,8,128]{2,1,0:T(8,128)S(1)} all-to-all(f32[16,8,128]{2,1,0:T(8,128)S(1)} %get-tuple-element.17), channel_id=1, replica_groups=mesh['rows_0'=4,'rows_1'=16,'cols_0'=4,'cols_1'=2] {'rows_1'}, dimensions={0} | all-to-all | bytes 131072 | tf_op jit(solution)/shard_map/all_to_all | solution.py:333
  28.6 19.4 %all_to_all.59 = f32[32,1,3200]{2,1,0:T(1,128)S(1)} all-to-all(f32[32,1,3200]{2,1,0:T(1,128)S(1)} %bitcast.16), channel_id=1, replica_groups=mesh['rows_0'=4,'rows_1'=16,'cols_0'=4,'cols_1'=2] {'rows_0','cols_0','c..., dimensions={0} | all-to-all | bytes 819200 | tf_op jit(solution)/shard_map/all_to_all | solution.py:333
  48.0 4.1 %first.1 = (bf16[4,512,512]{2,1,0:T(8,128)(2,1)S(1)}, f32[64,2176]{1,0:T(8,128)S(1)}, bf16[2048,1024]{1,0:T(8,128)(2,1)S(1)}, f32[16,16,128]{2,1,0:T(8,128)S(1)}) custom-call(f32[800,128]{1,0:T(8,128)S(1)} %bitcast.15, f32[16,8,128]{2,1,0:T(8,128)S(1)} %all_to_all.58.line_ref, f32[32]{0:T(128)} %noise_any.1), custom_call_target="tpu_custom_call" | custom-call | flops 1048576 | bytes 1048576 | tf_op jit(solution)/shard_map/first/pallas_call | solution.py:314
  52.2 15.1 %all_to_all.60.recv_ref = f32[16,16,128]{2,1,0:T(8,128)S(1)} all-to-all(f32[16,16,128]{2,1,0:T(8,128)S(1)} %get-tuple-element.18), channel_id=1, replica_groups=mesh['rows_0'=4,'rows_1'=16,'cols_0'=4,'cols_1'=2] {'rows_1'}, dimensions={0} | all-to-all | bytes 262144 | tf_op jit(solution)/shard_map/all_to_all | solution.py:333
  67.3 0.1 share.1
  67.4 14.7 %all_to_all.61.recv_ref.near_ref = f32[32,16,128]{2,1,0:T(8,128)S(1)} all-to-all(f32[32,16,128]{2,1,0:T(8,128)S(1)} %share.1), channel_id=1, replica_groups=mesh['rows_0'=4,'rows_1'=16,'cols_0'=4,'cols_1'=2] {'rows_0','cols_0','c..., dimensions={0} | all-to-all | bytes 524288 | tf_op jit(solution)/shard_map/all_to_all | solution.py:333
  82.1 0.3 sums.1
  82.4 15.2 %all_to_all.62 = f32[16,1,128]{2,1,0:T(1,128)S(1)} all-to-all(f32[16,1,128]{2,1,0:T(1,128)S(1)} %bitcast.22), channel_id=1, replica_groups=mesh['rows_0'=4,'rows_1'=16,'cols_0'=4,'cols_1'=2] {'rows_1'}, dimensions={0} | all-to-all | bytes 16384 | tf_op jit(solution)/shard_map/all_to_all | solution.py:333
  97.6 2.3 %second.1 = (f32[16,16,128]{2,1,0:T(8,128)S(1)}, f32[16,128]{1,0:T(8,128)S(1)}, f32[16,128]{1,0:T(8,128)S(1)}, f32[16,128]{1,0:T(8,128)S(1)}) custom-call(f32[16,128]{1,0:T(8,128)S(1)} %bitcast.20, f32[32,2048]{1,0:T(8,128)S(1)} %get-tuple-element.21.applied_ref, f32[64,2176]{1,0:T(8,128)S(1)} %get-tuple-element.19.state_ref, ...), custom_call_target="tpu_custom_call" | custom-call | flops 1048576 | bytes 1048576 | tf_op jit(solution)/shard_map/second/pallas_call | solution.py:314
  99.8 14.5 %all_to_all.63.recv_ref = f32[16,16,128]{2,1,0:T(8,128)S(1)} all-to-all(f32[16,16,128]{2,1,0:T(8,128)S(1)} %get-tuple-element.24), channel_id=1, replica_groups=mesh['rows_0'=4,'rows_1'=16,'cols_0'=4,'cols_1'=2] {'rows_1'}, dimensions={0} | all-to-all | bytes 262144 | tf_op jit(solution)/shard_map/all_to_all | solution.py:333
  114.4 0.3 last_sums.1
  114.7 13.7 %all_to_all.64 = f32[32,1,128]{2,1,0:T(1,128)S(1)} all-to-all(f32[32,1,128]{2,1,0:T(1,128)S(1)} %bitcast.21), channel_id=1, replica_groups=mesh['rows_0'=4,'rows_1'=16,'cols_0'=4,'cols_1'=2] {'rows_0','cols_0','c..., dimensions={0} | all-to-all | bytes 32768 | tf_op jit(solution)/shard_map/all_to_all | solution.py:333
  128.5 14.7 %all_to_all.65 = f32[16,1,128]{2,1,0:T(1,128)S(1)} all-to-all(f32[16,1,128]{2,1,0:T(1,128)S(1)} %bitcast.19), channel_id=1, replica_groups=mesh['rows_0'=4,'rows_1'=16,'cols_0'=4,'cols_1'=2] {'rows_1'}, dimensions={0} | all-to-all | bytes 16384 | tf_op jit(solution)/shard_map/all_to_all | solution.py:333
  143.1 0.8 end.1
  (1 shorter events, 0.0 us)

commit v7 on v5

--- a/solution.py
+++ b/solution.py
@@ -8,7 +8,7 @@
 
 INNER = 3
 X, Z, Y, K = "rows_0", "rows_1", "cols_0", "cols_1"
-ROWS, COLS, PLANE = (X, Z), (Y, K), (X, Y, K)
+PLANE = (X, Y, K)
 ROWS_COLS = (X, Z, Y, K)
 N_X, N_Z, N_C = 4, 16, 8
 FEATS, RHS, OWN, BLOCK = 16, 32, 64, 512
@@ -397,16 +397,16 @@
     line = swap(line_msg, Z)
     near_msg, applied = call(
         last_sums_body,
-        [((N_C, 128), F32), (packed, F32)],
+        [((n_p, 128), F32), (packed, F32)],
         line,
         corr_2,
         state,
         mine,
         name="last_sums",
     )
-    near = swap(near_msg, COLS)
-    (sums_msg,) = call(gather_body, [((N_X * N_Z, 128), F32)], near, name="near")
-    sums = swap(sums_msg, ROWS)
+    near = swap(near_msg, PLANE)
+    (sums_msg,) = call(gather_body, [((N_Z, 128), F32)], near, name="near")
+    sums = swap(sums_msg, Z)
     return tuple(
         call(
             end_body,

time: 145 us -> 144 us (level)
  no operation moved by 1% of the time
where the time goes in v7:
time: 144 us
  blocking collectives  110 us (76%)
  starting transfers between devices  13.1 us (9%)
  Pallas kernels  11.3 us (8%)
  waiting for transfers between devices  7.65 us (5%)
    all_to_all x7, blocking collectives, swap(): return lax.all_to_all(array, axis, split_axis=0, concat_axis=0, tiled=True)  110 us
    all_to_all x1, starting transfers between devices, swap(): return lax.all_to_all(array, axis, split_axis=0, concat_axis=0, tiled=True)  13.1 us
    pallas_call x9, Pallas kernels, call(): pl.pallas_call(body, out_shape=[jax.ShapeDtypeStruct(s, d) for s, d in ou...  11.3 us
    all_to_all x1, waiting for transfers between devices, swap(): return lax.all_to_all(array, axis, split_axis=0, concat_axis=0, tiled=True)  7.65 us
  transfers between devices with their start and end apart: 1, of which 1 were waited for; matrix products, arithmetic and copies ran while one was open for 0% of the time, Pallas kernels for 2%

profile of v7, /device:TPU:1, one launch (start us, length us, event | category | flops | bytes accessed | tf_op | source)
XLA Modules:
  0.0 143.7 jit_solution(5753847647973816278)
XLA Ops:
  0.6 1.5 %pack.1 = (f32[800,128]{1,0:T(8,128)S(1)}, f32[16,8,128]{2,1,0:T(8,128)}) custom-call(f32[16,64]{1,0:T(8,128)} %feat_any.1, f32[32,64]{1,0:T(8,128)} %targ_any.1, s32[1,64]{1,0:T(1,128)} %bitcast.23, f32[16]{0:T(128)} %scale_any.1), custom_call_target="tpu_custom_call" | custom-call | flops 1048576 | bytes 1048576 | tf_op jit(solution)/shard_map/pack/pallas_call | solution.py:314
  2.1 20.7 %all_to_all.58 = f32[32,1,3200]{2,1,0:T(1,128)} all-to-all(f32[32,1,3200]{2,1,0:T(1,128)S(1)} %bitcast.16), channel_id=1, replica_groups=mesh['rows_0'=4,'rows_1'=16,'cols_0'=4,'cols_1'=2] {'rows_0','cols_0','c..., dimensions={0} | all-to-all | bytes 819200 | tf_op jit(solution)/shard_map/all_to_all | solution.py:333
  22.8 13.1 %all-to-all-start = ((f32[16,8,128]{2,1,0:T(8,128)}), f32[16,8,128]{2,1,0:T(8,128)S(1)}, u32[]{:S(2)}, u32[]{:S(2)}) async-start(f32[16,8,128]{2,1,0:T(8,128)} %get-tuple-element.17), calls=%async_computation | async-start | bytes 131072 | tf_op jit(solution)/shard_map/all_to_all | solution.py:333
  36.0 0.0 copy-start
  36.0 1.0 copy-done
  37.0 2.9 %first.1 = (bf16[4,512,512]{2,1,0:T(8,128)(2,1)S(1)}, f32[64,2176]{1,0:T(8,128)S(1)}, bf16[2048,112]{1,0:T(8,128)(2,1)S(1)}) custom-call(f32[800,128]{1,0:T(8,128)S(1)} %bitcast.15, f32[32]{0:T(128)} %noise_any.1), custom_call_target="tpu_custom_call" | custom-call | flops 2147483648 | bytes 1048576 | tf_op jit(solution)/shard_map/first/pallas_call | solution.py:314
  39.9 7.7 %all-to-all-done.line_ref = f32[16,8,128]{2,1,0:T(8,128)S(1)} async-done(((f32[16,8,128]{2,1,0:T(8,128)}), f32[16,8,128]{2,1,0:T(8,128)S(1)}, u32[]{:S(2)}, u32[]{:S(2)}) %all-to-all-start) | async-done | bytes 65568 | tf_op jit(solution)/shard_map/all_to_all | solution.py:333
  47.6 3.0 %build.1 = (f32[16,16,128]{2,1,0:T(8,128)S(1)}, bf16[2048,1024]{1,0:T(8,128)(2,1)S(1)}) custom-call(f32[16,8,128]{2,1,0:T(8,128)S(1)} %all-to-all-done.line_ref, bf16[2048,112]{1,0:T(8,128)(2,1)S(1)} %get-tuple-element.19.left_ref, f32[64,2176]{1,0:T(8,128)S(1)} %get-tuple-element.20.state_ref), custom_call_target="tpu_custom_call" | custom-call | flops 1048576 | bytes 1048576 | tf_op jit(solution)/shard_map/build/pallas_call | solution.py:314
  50.6 15.9 %all_to_all.59.recv_ref = f32[16,16,128]{2,1,0:T(8,128)S(1)} all-to-all(f32[16,16,128]{2,1,0:T(8,128)S(1)} %get-tuple-element.21), channel_id=1, replica_groups=mesh['rows_0'=4,'rows_1'=16,'cols_0'=4,'cols_1'=2] {'rows_1'}, dimensions={0} | all-to-all | bytes 262144 | tf_op jit(solution)/shard_map/all_to_all | solution.py:333
  66.4 0.1 share.1
  66.5 15.9 %all_to_all.60.recv_ref.near_ref = f32[32,16,128]{2,1,0:T(8,128)S(1)} all-to-all(f32[32,16,128]{2,1,0:T(8,128)S(1)} %share.1), channel_id=1, replica_groups=mesh['rows_0'=4,'rows_1'=16,'cols_0'=4,'cols_1'=2] {'rows_0','cols_0','c..., dimensions={0} | all-to-all | bytes 524288 | tf_op jit(solution)/shard_map/all_to_all | solution.py:333
  82.4 0.3 sums.1
  82.7 14.6 %all_to_all.61 = f32[16,1,128]{2,1,0:T(1,128)S(1)} all-to-all(f32[16,1,128]{2,1,0:T(1,128)S(1)} %bitcast.22), channel_id=1, replica_groups=mesh['rows_0'=4,'rows_1'=16,'cols_0'=4,'cols_1'=2] {'rows_1'}, dimensions={0} | all-to-all | bytes 16384 | tf_op jit(solution)/shard_map/all_to_all | solution.py:333
  97.3 2.3 %second.1 = (f32[16,16,128]{2,1,0:T(8,128)S(1)}, f32[16,128]{1,0:T(8,128)S(1)}, f32[16,128]{1,0:T(8,128)S(1)}, f32[16,128]{1,0:T(8,128)S(1)}) custom-call(f32[16,128]{1,0:T(8,128)S(1)} %bitcast.20, f32[32,2048]{1,0:T(8,128)S(1)} %get-tuple-element.23.applied_ref, f32[64,2176]{1,0:T(8,128)S(1)} %get-tuple-element.20.state_ref, ...), custom_call_target="tpu_custom_call" | custom-call | flops 1048576 | bytes 1048576 | tf_op jit(solution)/shard_map/second/pallas_call | solution.py:314
  99.6 14.5 %all_to_all.62.recv_ref = f32[16,16,128]{2,1,0:T(8,128)S(1)} all-to-all(f32[16,16,128]{2,1,0:T(8,128)S(1)} %get-tuple-element.26), channel_id=1, replica_groups=mesh['rows_0'=4,'rows_1'=16,'cols_0'=4,'cols_1'=2] {'rows_1'}, dimensions={0} | all-to-all | bytes 262144 | tf_op jit(solution)/shard_map/all_to_all | solution.py:333
  114.1 0.3 last_sums.1
  114.4 13.7 %all_to_all.63 = f32[32,1,128]{2,1,0:T(1,128)S(1)} all-to-all(f32[32,1,128]{2,1,0:T(1,128)S(1)} %bitcast.21), channel_id=1, replica_groups=mesh['rows_0'=4,'rows_1'=16,'cols_0'=4,'cols_1'=2] {'rows_0','cols_0','c..., dimensions={0} | all-to-all | bytes 32768 | tf_op jit(solution)/shard_map/all_to_all | solution.py:333
  128.2 14.7 %all_to_all.64 = f32[16,1,128]{2,1,0:T(1,128)S(1)} all-to-all(f32[16,1,128]{2,1,0:T(1,128)S(1)} %bitcast.19), channel_id=1, replica_groups=mesh['rows_0'=4,'rows_1'=16,'cols_0'=4,'cols_1'=2] {'rows_1'}, dimensions={0} | all-to-all | bytes 16384 | tf_op jit(solution)/shard_map/all_to_all | solution.py:333
  142.9 0.8 end.1
  (1 shorter events, 0.0 us)
Async XLA Ops:
  22.8 24.7 %all-to-all-start = ((f32[16,8,128]{2,1,0:T(8,128)}), f32[16,8,128]{2,1,0:T(8,128)S(1)}, u32[]{:S(2)}, u32[]{:S(2)}) async-start(f32[16,8,128]{2,1,0:T(8,128)} %get-tuple-element.17), calls=%async_computation | async-start | bytes 131072 | tf_op jit(solution)/shard_map/all_to_all | solution.py:333
  36.0 1.0 copy-start

commit v8 on v7

--- a/solution.py
+++ b/solution.py
@@ -397,16 +397,16 @@
     line = swap(line_msg, Z)
     near_msg, applied = call(
         last_sums_body,
-        [((n_p, 128), F32), (packed, F32)],
+        [((n_p // 2, 128), F32), (packed, F32)],
         line,
         corr_2,
         state,
         mine,
         name="last_sums",
     )
-    near = swap(near_msg, PLANE)
-    (sums_msg,) = call(gather_body, [((N_Z, 128), F32)], near, name="near")
-    sums = swap(sums_msg, Z)
+    near = swap(near_msg, (X, Y))
+    (sums_msg,) = call(gather_body, [((2 * N_Z, 128), F32)], near, name="near")
+    sums = swap(sums_msg, (Z, K))
     return tuple(
         call(
             end_body,

time: 144 us -> 146 us (1.014)
  no operation moved by 1% of the time
where the time goes in v8:
time: 146 us; the launch traced here: 145 us
  blocking collectives  111 us (76%)
  starting transfers between devices  13.1 us (9%)
  Pallas kernels  11.3 us (8%)
  waiting for transfers between devices  7.65 us (5%)
    all_to_all x7, blocking collectives, swap(): return lax.all_to_all(array, axis, split_axis=0, concat_axis=0, tiled=True)  111 us
    all_to_all x1, starting transfers between devices, swap(): return lax.all_to_all(array, axis, split_axis=0, concat_axis=0, tiled=True)  13.1 us
    pallas_call x9, Pallas kernels, call(): pl.pallas_call(body, out_shape=[jax.ShapeDtypeStruct(s, d) for s, d in ou...  11.3 us
    all_to_all x1, waiting for transfers between devices, swap(): return lax.all_to_all(array, axis, split_axis=0, concat_axis=0, tiled=True)  7.65 us
  transfers between devices with their start and end apart: 1, of which 1 were waited for; matrix products, arithmetic and copies ran while one was open for 0% of the time, Pallas kernels for 2%

profile of v8, /device:TPU:1, one launch (start us, length us, event | category | flops | bytes accessed | tf_op | source)
XLA Modules:
  0.0 145.1 jit_solution(1522153153952401806)
XLA Ops:
  0.6 1.5 %pack.1 = (f32[800,128]{1,0:T(8,128)S(1)}, f32[16,8,128]{2,1,0:T(8,128)}) custom-call(f32[16,64]{1,0:T(8,128)} %feat_any.1, f32[32,64]{1,0:T(8,128)} %targ_any.1, s32[1,64]{1,0:T(1,128)} %bitcast.23, f32[16]{0:T(128)} %scale_any.1), custom_call_target="tpu_custom_call" | custom-call | flops 1048576 | bytes 1048576 | tf_op jit(solution)/shard_map/pack/pallas_call | solution.py:314
  2.1 20.7 %all_to_all.58 = f32[32,1,3200]{2,1,0:T(1,128)} all-to-all(f32[32,1,3200]{2,1,0:T(1,128)S(1)} %bitcast.16), channel_id=1, replica_groups=mesh['rows_0'=4,'rows_1'=16,'cols_0'=4,'cols_1'=2] {'rows_0','cols_0','c..., dimensions={0} | all-to-all | bytes 819200 | tf_op jit(solution)/shard_map/all_to_all | solution.py:333
  22.8 13.1 %all-to-all-start = ((f32[16,8,128]{2,1,0:T(8,128)}), f32[16,8,128]{2,1,0:T(8,128)S(1)}, u32[]{:S(2)}, u32[]{:S(2)}) async-start(f32[16,8,128]{2,1,0:T(8,128)} %get-tuple-element.17), calls=%async_computation | async-start | bytes 131072 | tf_op jit(solution)/shard_map/all_to_all | solution.py:333
  36.0 0.0 copy-start
  36.0 1.0 copy-done
  37.0 2.9 %first.1 = (bf16[4,512,512]{2,1,0:T(8,128)(2,1)S(1)}, f32[64,2176]{1,0:T(8,128)S(1)}, bf16[2048,112]{1,0:T(8,128)(2,1)S(1)}) custom-call(f32[800,128]{1,0:T(8,128)S(1)} %bitcast.15, f32[32]{0:T(128)} %noise_any.1), custom_call_target="tpu_custom_call" | custom-call | flops 2147483648 | bytes 1048576 | tf_op jit(solution)/shard_map/first/pallas_call | solution.py:314
  39.9 7.7 %all-to-all-done.line_ref = f32[16,8,128]{2,1,0:T(8,128)S(1)} async-done(((f32[16,8,128]{2,1,0:T(8,128)}), f32[16,8,128]{2,1,0:T(8,128)S(1)}, u32[]{:S(2)}, u32[]{:S(2)}) %all-to-all-start) | async-done | bytes 65568 | tf_op jit(solution)/shard_map/all_to_all | solution.py:333
  47.6 3.0 %build.1 = (f32[16,16,128]{2,1,0:T(8,128)S(1)}, bf16[2048,1024]{1,0:T(8,128)(2,1)S(1)}) custom-call(f32[16,8,128]{2,1,0:T(8,128)S(1)} %all-to-all-done.line_ref, bf16[2048,112]{1,0:T(8,128)(2,1)S(1)} %get-tuple-element.19.left_ref, f32[64,2176]{1,0:T(8,128)S(1)} %get-tuple-element.20.state_ref), custom_call_target="tpu_custom_call" | custom-call | flops 1048576 | bytes 1048576 | tf_op jit(solution)/shard_map/build/pallas_call | solution.py:314
  50.6 15.9 %all_to_all.59.recv_ref = f32[16,16,128]{2,1,0:T(8,128)S(1)} all-to-all(f32[16,16,128]{2,1,0:T(8,128)S(1)} %get-tuple-element.21), channel_id=1, replica_groups=mesh['rows_0'=4,'rows_1'=16,'cols_0'=4,'cols_1'=2] {'rows_1'}, dimensions={0} | all-to-all | bytes 262144 | tf_op jit(solution)/shard_map/all_to_all | solution.py:333
  66.4 0.1 share.1
  66.5 15.9 %all_to_all.60.recv_ref.near_ref = f32[32,16,128]{2,1,0:T(8,128)S(1)} all-to-all(f32[32,16,128]{2,1,0:T(8,128)S(1)} %share.1), channel_id=1, replica_groups=mesh['rows_0'=4,'rows_1'=16,'cols_0'=4,'cols_1'=2] {'rows_0','cols_0','c..., dimensions={0} | all-to-all | bytes 524288 | tf_op jit(solution)/shard_map/all_to_all | solution.py:333
  82.4 0.3 sums.1
  82.7 14.6 %all_to_all.61 = f32[16,1,128]{2,1,0:T(1,128)S(1)} all-to-all(f32[16,1,128]{2,1,0:T(1,128)S(1)} %bitcast.22), channel_id=1, replica_groups=mesh['rows_0'=4,'rows_1'=16,'cols_0'=4,'cols_1'=2] {'rows_1'}, dimensions={0} | all-to-all | bytes 16384 | tf_op jit(solution)/shard_map/all_to_all | solution.py:333
  97.3 2.3 %second.1 = (f32[16,16,128]{2,1,0:T(8,128)S(1)}, f32[16,128]{1,0:T(8,128)S(1)}, f32[16,128]{1,0:T(8,128)S(1)}, f32[16,128]{1,0:T(8,128)S(1)}) custom-call(f32[16,128]{1,0:T(8,128)S(1)} %bitcast.20, f32[32,2048]{1,0:T(8,128)S(1)} %get-tuple-element.23.applied_ref, f32[64,2176]{1,0:T(8,128)S(1)} %get-tuple-element.20.state_ref, ...), custom_call_target="tpu_custom_call" | custom-call | flops 1048576 | bytes 1048576 | tf_op jit(solution)/shard_map/second/pallas_call | solution.py:314
  99.6 14.5 %all_to_all.62.recv_ref = f32[16,16,128]{2,1,0:T(8,128)S(1)} all-to-all(f32[16,16,128]{2,1,0:T(8,128)S(1)} %get-tuple-element.26), channel_id=1, replica_groups=mesh['rows_0'=4,'rows_1'=16,'cols_0'=4,'cols_1'=2] {'rows_1'}, dimensions={0} | all-to-all | bytes 262144 | tf_op jit(solution)/shard_map/all_to_all | solution.py:333
  114.1 0.3 last_sums.1
  114.4 9.2 %all_to_all.63 = f32[16,1,128]{2,1,0:T(1,128)S(1)} all-to-all(f32[16,1,128]{2,1,0:T(1,128)S(1)} %bitcast.21), channel_id=1, replica_groups=mesh['rows_0'=4,'rows_1'=16,'cols_0'=4,'cols_1'=2] {'rows_0','cols_0'}, dimensions={0} | all-to-all | bytes 16384 | tf_op jit(solution)/shard_map/all_to_all | solution.py:333
  123.6 20.6 %all_to_all.64 = f32[32,1,128]{2,1,0:T(1,128)S(1)} all-to-all(f32[32,1,128]{2,1,0:T(1,128)S(1)} %bitcast.18), channel_id=1, replica_groups=mesh['rows_0'=4,'rows_1'=16,'cols_0'=4,'cols_1'=2] {'rows_1','cols_1'}, dimensions={0} | all-to-all | bytes 32768 | tf_op jit(solution)/shard_map/all_to_all | solution.py:333
  144.2 0.9 end.1
  (1 shorter events, 0.0 us)
Async XLA Ops:
  22.8 24.7 %all-to-all-start = ((f32[16,8,128]{2,1,0:T(8,128)}), f32[16,8,128]{2,1,0:T(8,128)S(1)}, u32[]{:S(2)}, u32[]{:S(2)}) async-start(f32[16,8,128]{2,1,0:T(8,128)} %get-tuple-element.17), calls=%async_computation | async-start | bytes 131072 | tf_op jit(solution)/shard_map/all_to_all | solution.py:333
  36.0 1.0 copy-start

commit v9 on v7

--- a/solution.py
+++ b/solution.py
@@ -158,7 +158,7 @@
 def pack_body(
     feat_any, targ_any, order_any, scale_any,
     plane_ref, line_ref,
-    feat_ref, targ_ref, order_ref, scale_ref, sems,
+    feat_ref, targ_ref, order_ref, scale_ref, copies_ref, sems,
 ):
     pairs = (
         (scale_any, scale_ref),
@@ -171,21 +171,26 @@
     ]
     for copy in copies:
         copy.start()
-    for copy in copies:
-        copy.wait()
 
     def halves(field):
         half = field.shape[0] // 2
         return jnp.concatenate([field[:half], field[half:]], axis=1)
 
+    copies[0].wait()
+    copies[1].wait()
     scaled = halves(feat_ref[...] / column(scale_ref, (FEATS, OWN)) * ROOT_LOG2E)
+    for to in range(N_Z):
+        copies_ref[to] = scaled
+    out = pltpu.make_async_copy(copies_ref, line_ref, sems.at[4])
+    out.start()
+    copies[2].wait()
+    copies[3].wait()
     order = (order_ref[...] % BLOCK).astype(F32)
     order = jnp.concatenate([order, order], axis=1)
     whole = jnp.concatenate([scaled, halves(targ_ref[...]), order], axis=0)
     for to in range(N_X * N_C):
         plane_ref[pl.ds(SENT * to, SENT), :] = whole
-    for to in range(N_Z):
-        line_ref[to] = scaled
+    out.wait()
 
 
 def cut(field, which):
@@ -310,14 +315,16 @@
     res_out[...] = split_halves(mine_ref[...] - damping * applied_ref[...])
 
 
-def call(body, outs, *args, scratch=(), spaces=None, flops=1 << 20, name):
+def call(body, outs, *args, scratch=(), spaces=None, out_spaces=None, flops=1 << 20, name):
     return pl.pallas_call(
         body,
         out_shape=[jax.ShapeDtypeStruct(s, d) for s, d in outs],
         in_specs=[
             pl.BlockSpec(memory_space=s) for s in spaces or (pltpu.VMEM,) * len(args)
         ],
-        out_specs=[pl.BlockSpec(memory_space=pltpu.VMEM)] * len(outs),
+        out_specs=[
+            pl.BlockSpec(memory_space=s) for s in out_spaces or (pltpu.VMEM,) * len(outs)
+        ],
         scratch_shapes=list(scratch),
         compiler_params=PARAMS,
         cost_estimate=pl.CostEstimate(flops=flops, transcendentals=0, bytes_accessed=1 << 20),
@@ -345,9 +352,11 @@
             pltpu.VMEM((RHS, OWN), F32),
             pltpu.VMEM((1, OWN), jnp.int32),
             pltpu.SMEM((FEATS,), F32),
-            pltpu.SemaphoreType.DMA((4,)),
+            pltpu.VMEM((N_Z, FEATS // 2, 2 * OWN), F32),
+            pltpu.SemaphoreType.DMA((5,)),
         ],
         spaces=(pltpu.HBM,) * 4,
+        out_spaces=(pltpu.VMEM, pltpu.HBM),
         name="pack",
     )
     plane = swap(plane_msg.reshape(n_p, 1, SENT * 128), PLANE).reshape(n_p * SENT, 128)

time: 144 us -> 144 us (level)
  no operation moved by 1% of the time
where the time goes in v9:
time: 144 us
  blocking collectives  110 us (76%)
  starting transfers between devices  13.1 us (9%)
  Pallas kernels  11.2 us (8%)
  waiting for transfers between devices  7.65 us (5%)
    all_to_all x7, blocking collectives, swap(): return lax.all_to_all(array, axis, split_axis=0, concat_axis=0, tiled=True)  110 us
    all_to_all x1, starting transfers between devices, swap(): return lax.all_to_all(array, axis, split_axis=0, concat_axis=0, tiled=True)  13.1 us
    pallas_call x9, Pallas kernels, call(): pl.pallas_call(body, out_shape=[jax.ShapeDtypeStruct(s, d) for s, d in ou...  11.2 us
    all_to_all x1, waiting for transfers between devices, swap(): return lax.all_to_all(array, axis, split_axis=0, concat_axis=0, tiled=True)  7.65 us
  transfers between devices with their start and end apart: 1, of which 1 were waited for; matrix products, arithmetic and copies ran while one was open for 0% of the time, Pallas kernels for 2%

profile of v9, /device:TPU:1, one launch (start us, length us, event | category | flops | bytes accessed | tf_op | source)
XLA Modules:
  0.0 143.7 jit_solution(14180932571989679546)
XLA Ops:
  0.6 1.4 %pack.1 = (f32[800,128]{1,0:T(8,128)S(1)}, f32[16,8,128]{2,1,0:T(8,128)}) custom-call(f32[16,64]{1,0:T(8,128)} %feat_any.1, f32[32,64]{1,0:T(8,128)} %targ_any.1, s32[1,64]{1,0:T(1,128)} %bitcast.23, f32[16]{0:T(128)} %scale_any.1), custom_call_target="tpu_custom_call" | custom-call | flops 1048576 | bytes 1048576 | tf_op jit(solution)/shard_map/pack/pallas_call | solution.py:319
  2.1 20.7 %all_to_all.58 = f32[32,1,3200]{2,1,0:T(1,128)} all-to-all(f32[32,1,3200]{2,1,0:T(1,128)S(1)} %bitcast.16), channel_id=1, replica_groups=mesh['rows_0'=4,'rows_1'=16,'cols_0'=4,'cols_1'=2] {'rows_0','cols_0','c..., dimensions={0} | all-to-all | bytes 819200 | tf_op jit(solution)/shard_map/all_to_all | solution.py:340
  22.8 13.1 %all-to-all-start = ((f32[16,8,128]{2,1,0:T(8,128)}), f32[16,8,128]{2,1,0:T(8,128)S(1)}, u32[]{:S(2)}, u32[]{:S(2)}) async-start(f32[16,8,128]{2,1,0:T(8,128)} %get-tuple-element.17), calls=%async_computation | async-start | bytes 131072 | tf_op jit(solution)/shard_map/all_to_all | solution.py:340
  35.9 0.0 copy-start
  35.9 1.0 copy-done
  36.9 2.9 %first.1 = (bf16[4,512,512]{2,1,0:T(8,128)(2,1)S(1)}, f32[64,2176]{1,0:T(8,128)S(1)}, bf16[2048,112]{1,0:T(8,128)(2,1)S(1)}) custom-call(f32[800,128]{1,0:T(8,128)S(1)} %bitcast.15, f32[32]{0:T(128)} %noise_any.1), custom_call_target="tpu_custom_call" | custom-call | flops 2147483648 | bytes 1048576 | tf_op jit(solution)/shard_map/first/pallas_call | solution.py:319
  39.9 7.7 %all-to-all-done.line_ref = f32[16,8,128]{2,1,0:T(8,128)S(1)} async-done(((f32[16,8,128]{2,1,0:T(8,128)}), f32[16,8,128]{2,1,0:T(8,128)S(1)}, u32[]{:S(2)}, u32[]{:S(2)}) %all-to-all-start) | async-done | bytes 65568 | tf_op jit(solution)/shard_map/all_to_all | solution.py:340
  47.5 3.0 %build.1 = (f32[16,16,128]{2,1,0:T(8,128)S(1)}, bf16[2048,1024]{1,0:T(8,128)(2,1)S(1)}) custom-call(f32[16,8,128]{2,1,0:T(8,128)S(1)} %all-to-all-done.line_ref, bf16[2048,112]{1,0:T(8,128)(2,1)S(1)} %get-tuple-element.19.left_ref, f32[64,2176]{1,0:T(8,128)S(1)} %get-tuple-element.20.state_ref), custom_call_target="tpu_custom_call" | custom-call | flops 1048576 | bytes 1048576 | tf_op jit(solution)/shard_map/build/pallas_call | solution.py:319
  50.5 15.9 %all_to_all.59.recv_ref = f32[16,16,128]{2,1,0:T(8,128)S(1)} all-to-all(f32[16,16,128]{2,1,0:T(8,128)S(1)} %get-tuple-element.21), channel_id=1, replica_groups=mesh['rows_0'=4,'rows_1'=16,'cols_0'=4,'cols_1'=2] {'rows_1'}, dimensions={0} | all-to-all | bytes 262144 | tf_op jit(solution)/shard_map/all_to_all | solution.py:340
  66.4 0.1 share.1
  66.5 15.9 %all_to_all.60.recv_ref.near_ref = f32[32,16,128]{2,1,0:T(8,128)S(1)} all-to-all(f32[32,16,128]{2,1,0:T(8,128)S(1)} %share.1), channel_id=1, replica_groups=mesh['rows_0'=4,'rows_1'=16,'cols_0'=4,'cols_1'=2] {'rows_0','cols_0','c..., dimensions={0} | all-to-all | bytes 524288 | tf_op jit(solution)/shard_map/all_to_all | solution.py:340
  82.3 0.3 sums.1
  82.7 14.6 %all_to_all.61 = f32[16,1,128]{2,1,0:T(1,128)S(1)} all-to-all(f32[16,1,128]{2,1,0:T(1,128)S(1)} %bitcast.22), channel_id=1, replica_groups=mesh['rows_0'=4,'rows_1'=16,'cols_0'=4,'cols_1'=2] {'rows_1'}, dimensions={0} | all-to-all | bytes 16384 | tf_op jit(solution)/shard_map/all_to_all | solution.py:340
  97.3 2.3 %second.1 = (f32[16,16,128]{2,1,0:T(8,128)S(1)}, f32[16,128]{1,0:T(8,128)S(1)}, f32[16,128]{1,0:T(8,128)S(1)}, f32[16,128]{1,0:T(8,128)S(1)}) custom-call(f32[16,128]{1,0:T(8,128)S(1)} %bitcast.20, f32[32,2048]{1,0:T(8,128)S(1)} %get-tuple-element.23.applied_ref, f32[64,2176]{1,0:T(8,128)S(1)} %get-tuple-element.20.state_ref, ...), custom_call_target="tpu_custom_call" | custom-call | flops 1048576 | bytes 1048576 | tf_op jit(solution)/shard_map/second/pallas_call | solution.py:319
  99.5 14.5 %all_to_all.62.recv_ref = f32[16,16,128]{2,1,0:T(8,128)S(1)} all-to-all(f32[16,16,128]{2,1,0:T(8,128)S(1)} %get-tuple-element.26), channel_id=1, replica_groups=mesh['rows_0'=4,'rows_1'=16,'cols_0'=4,'cols_1'=2] {'rows_1'}, dimensions={0} | all-to-all | bytes 262144 | tf_op jit(solution)/shard_map/all_to_all | solution.py:340
  114.1 0.3 last_sums.1
  114.4 13.7 %all_to_all.63 = f32[32,1,128]{2,1,0:T(1,128)S(1)} all-to-all(f32[32,1,128]{2,1,0:T(1,128)S(1)} %bitcast.21), channel_id=1, replica_groups=mesh['rows_0'=4,'rows_1'=16,'cols_0'=4,'cols_1'=2] {'rows_0','cols_0','c..., dimensions={0} | all-to-all | bytes 32768 | tf_op jit(solution)/shard_map/all_to_all | solution.py:340
  128.1 14.7 %all_to_all.64 = f32[16,1,128]{2,1,0:T(1,128)S(1)} all-to-all(f32[16,1,128]{2,1,0:T(1,128)S(1)} %bitcast.19), channel_id=1, replica_groups=mesh['rows_0'=4,'rows_1'=16,'cols_0'=4,'cols_1'=2] {'rows_1'}, dimensions={0} | all-to-all | bytes 16384 | tf_op jit(solution)/shard_map/all_to_all | solution.py:340
  142.8 0.8 end.1
  (1 shorter events, 0.0 us)
Async XLA Ops:
  22.8 24.7 %all-to-all-start = ((f32[16,8,128]{2,1,0:T(8,128)}), f32[16,8,128]{2,1,0:T(8,128)S(1)}, u32[]{:S(2)}, u32[]{:S(2)}) async-start(f32[16,8,128]{2,1,0:T(8,128)} %get-tuple-element.17), calls=%async_computation | async-start | bytes 131072 | tf_op jit(solution)/shard_map/all_to_all | solution.py:340
  35.9 1.0 copy-start
